TPU v7x, 128 devices: a whole 4x4x4 slice. The times are simulated.
128 devices in a mesh: slab: 64 (over z, y, x), row: 2 (over core).
Axes of the slice: x: 4, y: 4, z: 4, core: 2. Of those that a mesh axis runs over, the one named last changes fastest.
Arguments:
- diag_block: float32 [64, 2, 512, 512], P('slab', None, 'row'), may hold values from -3 to 8
- lower_block: float32 [64, 2, 512, 512], P('slab', None, 'row'), may hold values from -0.4375 to 0.4375
- upper_block: float32 [64, 2, 512, 512], P('slab', None, 'row'), may hold values from -0.4375 to 0.4375
- twist: int32 [64, 512], P('slab'), may hold values from 0 to 511, each once within a row
- excitation: float32 [64, 2, 512, 128], P('slab', None, 'row'), may hold values from -24 to 24
Outputs:
- solution: float32 [64, 2, 512, 128], P('slab', None, 'row')
Inputs may be any that keep to these rules, and one draw needn't show every extreme that they name: Each row of twist is a permutation of 0 to 511.
All inputs are finite; a program needn't handle non-finite values.
Results may differ from a plain program's by a relative error of at most 0.00014.
Values sent between devices are 32-bit elements; how exact they have to be, the bound alone decides.
A program may use at most 128 MiB of HBM per device.

v0:
```python
import jax
import jax.numpy as jnp
from jax import lax
from jax.sharding import PartitionSpec as P


def from_behind(x, axis, by):
    peers = lax.axis_size(axis)
    pairs = [(i, i + by) for i in range(peers) if 0 <= i + by < peers]
    return lax.ppermute(x, axis, pairs)


def complex_product(left_mat, right_mat):
    exact = lax.Precision.HIGHEST
    real_part = jnp.dot(
        left_mat[0], right_mat[0], precision=exact, preferred_element_type=jnp.float32
    ) - jnp.dot(left_mat[1], right_mat[1], precision=exact, preferred_element_type=jnp.float32)
    imag_part = jnp.dot(
        left_mat[0], right_mat[1], precision=exact, preferred_element_type=jnp.float32
    ) + jnp.dot(left_mat[1], right_mat[0], precision=exact, preferred_element_type=jnp.float32)
    return jnp.stack([real_part, imag_part])


def gather_square(block_rows):
    return lax.all_gather(block_rows, "row", axis=1, tiled=True)


def gather_couplings(upper_rows, lower_rows, drive_rows):
    return (
        lax.all_gather(upper_rows, "row", axis=1, tiled=True),
        lax.all_gather(lower_rows, "row", axis=1, tiled=True),
        lax.all_gather(drive_rows, "row", axis=1, tiled=True),
    )


def slab_neighbor(value, offset):
    return from_behind(value, "slab", offset)


def gather_solution(vector_rows):
    return lax.all_gather(vector_rows, "row", axis=1, tiled=True)


def newton_state(block_rows, row_start, need_full):
    row_count = block_rows.shape[1]
    block_full = gather_square(block_rows)
    order = block_full.shape[2]
    identity = (
        lax.broadcasted_iota(jnp.int32, (order, order), 0)
        == lax.broadcasted_iota(jnp.int32, (order, order), 1)
    ).astype(jnp.float32)
    iterate_full = jnp.stack([0.4 * identity - 0.04 * block_full[0], -0.04 * block_full[1]])
    iterate_rows = lax.dynamic_slice_in_dim(iterate_full, row_start, row_count, 1)
    update = complex_product(complex_product(iterate_rows, block_full), iterate_full)
    iterate_full = gather_square(2.0 * iterate_rows - update)
    iterate_rows = lax.dynamic_slice_in_dim(iterate_full, row_start, row_count, 1)
    product_rows = complex_product(iterate_rows, block_full)
    inverse_rows = 2.0 * iterate_rows - complex_product(product_rows, iterate_full)
    inverse_full = gather_square(inverse_rows) if need_full else inverse_rows
    return (inverse_rows, inverse_full, block_full, product_rows)


def left_apply(left_rows, inverse_state):
    return complex_product(left_rows, inverse_state[1])


def right_apply(inverse_state, vector_full):
    return complex_product(inverse_state[0], vector_full)


def neighbor_solutions(local_rows, distance):
    lower_side = gather_solution(slab_neighbor(local_rows, distance))
    upper_side = gather_solution(slab_neighbor(local_rows, -distance))
    return (lower_side, upper_side)


def body(diag_block, lower_block, upper_block, twist, excitation):
    slab_count = lax.axis_size("slab")
    slab_index = lax.axis_index("slab")
    row_index = lax.axis_index("row")
    diag_rows = diag_block[0]
    row_count = diag_rows.shape[1]
    order = diag_rows.shape[2]
    row_start = row_index * row_count
    strand_order = twist[0]
    lower_twisted = jnp.take(lower_block[0], strand_order, axis=2) * (slab_index > 0).astype(
        jnp.float32
    )
    upper_twisted = jnp.take(upper_block[0], strand_order, axis=2) * (
        slab_index < slab_count - 1
    ).astype(jnp.float32)
    drive_rows = excitation[0]
    even_slab = slab_index % 2 == 0
    fourth_slab = slab_index % 4 == 0
    first_state = newton_state(diag_rows, row_start, True)
    upper_full, lower_full, drive_full = gather_couplings(upper_twisted, lower_twisted, drive_rows)
    toward_upper = left_apply(slab_neighbor(lower_twisted, -1), first_state)
    toward_lower = left_apply(slab_neighbor(upper_twisted, 1), first_state)
    sent_upper = jnp.concatenate(
        [
            complex_product(toward_upper, upper_full),
            complex_product(toward_upper, lower_full),
            complex_product(toward_upper, drive_full),
        ],
        axis=2,
    )
    sent_lower = jnp.concatenate(
        [
            complex_product(toward_lower, upper_full),
            complex_product(toward_lower, lower_full),
            complex_product(toward_lower, drive_full),
        ],
        axis=2,
    )
    from_lower = slab_neighbor(sent_upper, 1)
    from_upper = slab_neighbor(sent_lower, -1)
    diag_one = jnp.where(
        even_slab,
        diag_rows - from_lower[:, :, :order] - from_upper[:, :, order : 2 * order],
        diag_rows,
    )
    lower_one = jnp.where(even_slab, -from_lower[:, :, order : 2 * order], lower_twisted)
    upper_one = jnp.where(even_slab, -from_upper[:, :, :order], upper_twisted)
    drive_one = jnp.where(
        even_slab,
        drive_rows - from_lower[:, :, 2 * order :] - from_upper[:, :, 2 * order :],
        drive_rows,
    )
    second_state = newton_state(diag_one, row_start, True)
    upper_two, lower_two, drive_two = gather_couplings(upper_one, lower_one, drive_one)
    toward_upper = left_apply(slab_neighbor(lower_one, -2), second_state)
    toward_lower = left_apply(slab_neighbor(upper_one, 2), second_state)
    sent_upper = jnp.concatenate(
        [complex_product(toward_upper, upper_two), complex_product(toward_upper, drive_two)], axis=2
    )
    sent_lower = jnp.concatenate(
        [complex_product(toward_lower, lower_two), complex_product(toward_lower, drive_two)], axis=2
    )
    from_lower = slab_neighbor(sent_upper, 2)
    from_upper = slab_neighbor(sent_lower, -2)
    diag_two = jnp.where(
        fourth_slab, diag_one - from_lower[:, :, :order] - from_upper[:, :, :order], diag_one
    )
    drive_coarse = jnp.where(
        fourth_slab, drive_one - from_lower[:, :, order:] - from_upper[:, :, order:], drive_one
    )
    coarse_state = newton_state(diag_two, row_start, False)
    coarse_solution = right_apply(coarse_state, gather_solution(drive_coarse))
    lower_side, upper_side = neighbor_solutions(coarse_solution, 2)
    middle_residual = (
        drive_two - complex_product(lower_two, lower_side) - complex_product(upper_two, upper_side)
    )
    middle_solution = right_apply(second_state, middle_residual)
    even_solution = jnp.where(fourth_slab, coarse_solution, middle_solution)
    lower_side, upper_side = neighbor_solutions(even_solution, 1)
    odd_residual = (
        drive_full
        - complex_product(lower_full, lower_side)
        - complex_product(upper_full, upper_side)
    )
    odd_solution = right_apply(first_state, odd_residual)
    return jnp.where(even_slab, even_solution, odd_solution)[None]


def solution(mesh):
    return jax.shard_map(
        body,
        mesh=mesh,
        in_specs=(
            P("slab", None, "row", None),
            P("slab", None, "row", None),
            P("slab", None, "row", None),
            P("slab", None),
            P("slab", None, "row", None),
        ),
        out_specs=P("slab", None, "row", None),
        check_vma=False,
    )
```

profile of v0, /device:TPU:33, one launch (start us, length us, event | category | flops | bytes accessed | tf_op | source)
XLA Modules:
  0.0 517.0 jit_solution(17051444374406451518)
XLA Ops:
  7.3 17.5 %all-gather.37.cloned.1.call-done = f32[1,2,512,512]{3,2,1,0:T(8,128)} async-done(((f32[1,2,256,512]{3,2,1,0:T(8,128)}), f32[1,2,512,512]{3,2,1,0:T(8,128)}) %all-gather.37.cloned.1.call-update) | async-done | bytes 2097168 | tf_op jit(solution)/shard_map/all_gather | solution.py:25
  37.1 14.5 %all-gather.15.cloned.1.call-done = f32[2,512,512]{2,1,0:T(8,128)} async-done(((f32[2,256,512]{2,1,0:T(8,128)}), f32[2,512,512]{2,1,0:T(8,128)}) %all-gather.15.cloned.1.call-update) | async-done | bytes 2097168 | tf_op jit(solution)/shard_map/all_gather | solution.py:25
  51.7 2.2 fusion.73
  63.3 3.1 gather_fusion
  69.3 3.2 gather_fusion.1
  72.5 1.6 copy.25
  74.2 2.7 bitcast_multiply_fusion.7
  76.9 6.5 %collective-permute-start = (f32[2,256,512]{2,1,0:T(8,128)}, f32[2,256,512]{2,1,0:T(8,128)S(1)}, u32[]{:S(2)}, u32[]{:S(2)}) collective-permute-start(f32[2,256,512]{2,1,0:T(8,128)} %get-tuple-element.13), channel_id=1, source_target_pairs={{2,0},{4,2},{6,4},{8,6},{10,8},{12,10},{14,12},{16,14},{18,16},{20... | collective-permute-start | bytes 3145736 | tf_op jit(solution)/shard_map/ppermute | solution.py:10
  83.4 1.9 collective-permute-start.2
  85.5 2.7 all-gather.1
  88.2 17.9 %collective-permute-done = f32[2,256,512]{2,1,0:T(8,128)S(1)} collective-permute-done((f32[2,256,512]{2,1,0:T(8,128)}, f32[2,256,512]{2,1,0:T(8,128)S(1)}, u32[]{:S(2)}, u32[]{:S(2)}) %collective-permute-start) | collective-permute-done | bytes 1048608 | tf_op jit(solution)/shard_map/ppermute | solution.py:10
  106.1 2.8 fusion.97
  112.2 2.1 convolution_add_fusion.17
  114.3 2.1 fusion.96
  116.4 2.1 convolution_subtract_fusion.14
  120.3 2.1 fusion.94
  122.4 2.1 convolution_add_fusion.14
  127.1 3.4 fusion.123
  130.5 2.9 fusion.119
  133.4 2.6 fusion.117
  136.0 2.1 fusion.113
  144.0 8.3 %collective-permute-start.3 = (f32[2,256,1152]{2,1,0:T(8,128)}, f32[2,256,1152]{2,1,0:T(8,128)}, u32[]{:S(2)}, u32[]{:S(2)}) collective-permute-start(f32[2,256,1152]{2,1,0:T(8,128)} %maximum_maximum_fusion.1), channel_id=1, source_target_pairs={{2,0},{4,2},{6,4},{8,6},{10,8},{12,10},{14,12},{16,14},{18,16},{20... | collective-permute-start | bytes 7077896 | tf_op jit(solution)/shard_map/ppermute | solution.py:10
  162.5 2.0 collective-permute-start.1
  164.6 37.4 %collective-permute-done.3 = f32[2,256,1152]{2,1,0:T(8,128)} collective-permute-done((f32[2,256,1152]{2,1,0:T(8,128)}, f32[2,256,1152]{2,1,0:T(8,128)}, u32[]{:S(2)}, u32[]{:S(2)}) %collective-permute-start.3) | collective-permute-done | bytes 2359328 | tf_op jit(solution)/shard_map/ppermute | solution.py:10
  202.0 18.5 %collective-permute-done.1 = f32[2,256,1152]{2,1,0:T(8,128)} collective-permute-done((f32[2,256,1152]{2,1,0:T(8,128)}, f32[2,256,1152]{2,1,0:T(8,128)}, u32[]{:S(2)}, u32[]{:S(2)}) %collective-permute-start.1) | collective-permute-done | bytes 2359328 | tf_op jit(solution)/shard_map/ppermute | solution.py:10
  220.5 4.3 fusion.47
  225.2 11.7 %all-gather.23.cloned.1.call-done = f32[2,512,512]{2,1,0:T(8,128)} async-done(((f32[2,256,512]{2,1,0:T(8,128)}), f32[2,512,512]{2,1,0:T(8,128)}) %all-gather.23.cloned.1.call-update) | async-done | bytes 2097168 | tf_op jit(solution)/shard_map/all_gather | solution.py:25
  236.9 1.8 slice_multiply_fusion.1
  250.7 14.3 %all-gather.25.cloned.1.call-done = f32[2,512,512]{2,1,0:T(8,128)} async-done(((f32[2,256,512]{2,1,0:T(8,128)}), f32[2,512,512]{2,1,0:T(8,128)}) %all-gather.25.cloned.1.call-update) | async-done | bytes 2097168 | tf_op jit(solution)/shard_map/all_gather | solution.py:25
  265.0 2.2 fusion.61
  276.7 6.7 %collective-permute-start.4 = (f32[2,256,512]{2,1,0:T(8,128)S(1)}, f32[2,256,512]{2,1,0:T(8,128)S(1)}, u32[]{:S(2)}, u32[]{:S(2)}) collective-permute-start(f32[2,256,512]{2,1,0:T(8,128)S(1)} %copy-done.35), channel_id=1, source_target_pairs={{4,0},{6,2},{8,4},{10,6},{12,8},{14,10},{16,12},{18,14},{20,16},{2... | collective-permute-start | bytes 3145736 | tf_op jit(solution)/shard_map/ppermute | solution.py:10
  283.4 1.9 collective-permute-start.6
  286.6 2.6 all_gather.67
  289.1 16.6 %collective-permute-done.4 = f32[2,256,512]{2,1,0:T(8,128)S(1)} collective-permute-done((f32[2,256,512]{2,1,0:T(8,128)S(1)}, f32[2,256,512]{2,1,0:T(8,128)S(1)}, u32[]{:S(2)}, u32[]{:S(2)}) %collective-permute-start.4) | collective-permute-done | bytes 1048608 | tf_op jit(solution)/shard_map/ppermute | solution.py:10
  306.7 2.6 fusion.101
  309.3 2.2 convolution_subtract_fusion.7
  314.4 2.6 fusion.102
  323.2 4.6 collective-permute-start.5
  329.3 2.1 fusion.100
  331.4 2.1 convolution_subtract_fusion.5
  334.1 2.1 fusion.98
  336.2 2.1 convolution_add_fusion.5
  340.7 2.6 fusion.109
  347.7 4.9 collective-permute-start.7
  352.6 6.7 %collective-permute-done.5 = f32[2,256,640]{2,1,0:T(8,128)} collective-permute-done((f32[2,256,640]{2,1,0:T(8,128)}, f32[2,256,640]{2,1,0:T(8,128)}, u32[]{:S(2)}, u32[]{:S(2)}) %collective-permute-start.5) | collective-permute-done | bytes 1310752 | tf_op jit(solution)/shard_map/ppermute | solution.py:10
  359.4 24.1 %collective-permute-done.7 = f32[2,256,640]{2,1,0:T(8,128)} collective-permute-done((f32[2,256,640]{2,1,0:T(8,128)}, f32[2,256,640]{2,1,0:T(8,128)}, u32[]{:S(2)}, u32[]{:S(2)}) %collective-permute-start.7) | collective-permute-done | bytes 1310752 | tf_op jit(solution)/shard_map/ppermute | solution.py:10
  383.5 2.9 fusion.45
  386.9 19.3 %all-gather.33.cloned.1.call-done = f32[2,512,512]{2,1,0:T(8,128)} async-done(((f32[2,256,512]{2,1,0:T(8,128)}), f32[2,512,512]{2,1,0:T(8,128)}) %all-gather.33.cloned.1.call-update) | async-done | bytes 2097168 | tf_op jit(solution)/shard_map/all_gather | solution.py:25
  406.2 1.8 slice_multiply_fusion
  420.7 2.4 all_gather.71
  423.0 11.3 %all-gather.35.cloned.1.call-done = f32[2,512,512]{2,1,0:T(8,128)} async-done(((f32[2,256,512]{2,1,0:T(8,128)}), f32[2,512,512]{2,1,0:T(8,128)}) %all-gather.35.cloned.1.call-update) | async-done | bytes 2097168 | tf_op jit(solution)/shard_map/all_gather | solution.py:25
  434.4 2.2 fusion.49
  446.7 6.7 %collective-permute-start.9 = (f32[2,256,128]{2,1,0:T(8,128)S(1)}, f32[2,256,128]{2,1,0:T(8,128)S(1)}, u32[]{:S(2)}, u32[]{:S(2)}) collective-permute-start(f32[2,256,128]{2,1,0:T(8,128)S(1)} %pad_maximum_fusion), channel_id=1, source_target_pairs={{4,0},{6,2},{8,4},{10,6},{12,8},{14,10},{16,12},{18,14},{20,16},{2... | collective-permute-start | bytes 786440 | tf_op jit(solution)/shard_map/ppermute | solution.py:10
  453.4 1.9 collective-permute-start.8
  455.3 3.5 collective-permute-done.9
  458.8 3.8 all_gather.73
  464.6 2.6 collective-permute-done.8
  467.2 3.2 all_gather.72
  478.9 4.8 collective-permute-start.11
  483.7 1.9 collective-permute-start.10
  485.7 3.3 collective-permute-done.11
  489.0 3.3 all_gather.75
  494.3 2.8 collective-permute-done.10
  497.1 3.3 all_gather.74
  (261 shorter events, 135.1 us)
Async XLA Ops:
  6.5 18.3 %all-gather.37.cloned.1.call-start = ((), (), s32[]{:S(2)}) async-start(), calls=%async_computation.11 | async-start | bytes 3145728 | tf_op jit(solution)/shard_map/all_gather | solution.py:25
  7.3 44.4 %all-gather.15.cloned.1.call-start = ((), (), s32[]{:S(2)}) async-start(), calls=%async_computation | async-start | bytes 3145728 | tf_op jit(solution)/shard_map/all_gather | solution.py:25
  24.8 1.9 copy-start
  36.9 69.2 %all-gather.17.cloned.1.call-start = ((), (), s32[]{:S(2)}) async-start(), calls=%async_computation.1 | async-start | bytes 3145728 | tf_op jit(solution)/shard_map/all_gather | solution.py:25
  51.6 2.2 copy-start.14
  61.3 1.4 copy-start.38
  62.6 64.5 %all-gather.21.cloned.1.call-start = ((), (), s32[]{:S(2)}) async-start(), calls=%async_computation.3 | async-start | bytes 3145728 | tf_op jit(solution)/shard_map/all_gather | solution.py:31
  66.4 1.6 copy-start.39
  76.8 8.6 %copy-start.29 = (f32[2,256,512]{2,1,0:T(8,128)}, f32[2,256,512]{2,1,0:T(8,128)S(1)}, u32[]{:S(2)}) copy-start(f32[2,256,512]{2,1,0:T(8,128)S(1)} %get-tuple-element.14) | copy-start | bytes 3145732
  76.8 8.6 %copy-start.40 = (f32[1,2,256,128]{3,2,1,0:T(8,128)S(1)}, f32[1,2,256,128]{3,2,1,0:T(8,128)}, u32[]{:S(2)}) copy-start(f32[1,2,256,128]{3,2,1,0:T(8,128)} %param.11) | copy-start | bytes 786436
  76.8 56.6 %all-gather.19.cloned.1.call-start = ((), (), s32[]{:S(2)}) async-start(), calls=%async_computation.2 | async-start | bytes 3145728 | tf_op jit(solution)/shard_map/all_gather | solution.py:30
  76.9 29.1 %collective-permute-start = (f32[2,256,512]{2,1,0:T(8,128)}, f32[2,256,512]{2,1,0:T(8,128)S(1)}, u32[]{:S(2)}, u32[]{:S(2)}) collective-permute-start(f32[2,256,512]{2,1,0:T(8,128)} %get-tuple-element.13), channel_id=1, source_target_pairs={{2,0},{4,2},{6,4},{8,6},{10,8},{12,10},{14,12},{16,14},{18,16},{20... | collective-permute-start | bytes 3145736 | tf_op jit(solution)/shard_map/ppermute | solution.py:10
  83.4 30.9 %collective-permute-start.2 = (f32[2,256,512]{2,1,0:T(8,128)S(1)}, f32[2,256,512]{2,1,0:T(8,128)}, u32[]{:S(2)}, u32[]{:S(2)}) collective-permute-start(f32[2,256,512]{2,1,0:T(8,128)S(1)} %get-tuple-element.14), channel_id=1, source_target_pairs={{0,2},{2,4},{4,6},{6,8},{8,10},{10,12},{12,14},{14,16},{16,18},{18... | collective-permute-start | bytes 3145736 | tf_op jit(solution)/shard_map/ppermute | solution.py:10
  85.4 151.5 %all-gather.23.cloned.1.call-start = ((), (), s32[]{:S(2)}) async-start(), calls=%async_computation.4 | async-start | bytes 3145728 | tf_op jit(solution)/shard_map/all_gather | solution.py:25
  88.2 37.5 %copy-start.19 = (f32[1,2,512,128]{3,2,1,0:T(8,128)}, f32[1,2,512,128]{3,2,1,0:T(8,128)S(1)}, u32[]{:S(2)}) copy-start(f32[1,2,512,128]{3,2,1,0:T(8,128)S(1)} %all-gather.1) | copy-start | bytes 1572868
  106.0 5.1 copy-start.31
  106.0 2.8 copy-start.11
  109.9 4.4 copy-start.16
  118.5 6.6 %copy-start.18 = (f32[256,512]{1,0:T(8,128)}, f32[256,512]{1,0:T(8,128)S(1)}, u32[]{:S(2)}) copy-start(f32[256,512]{1,0:T(8,128)S(1)} %convolution_subtract_fusion.14) | copy-start | bytes 1572868
  127.1 3.4 copy-start.3
  133.4 2.6 copy-start.5
  133.4 4.8 copy-start.37
  136.0 3.2 copy-start.36
  140.3 2.1 copy-start.42
  142.5 9.9 %copy-start.17 = (f32[256,512]{1,0:T(8,128)S(1)}, f32[256,512]{1,0:T(8,128)}, u32[]{:S(2)}) copy-start(f32[256,512]{1,0:T(8,128)} %copy-done.16) | copy-start | bytes 1572868
  144.0 58.0 %collective-permute-start.3 = (f32[2,256,1152]{2,1,0:T(8,128)}, f32[2,256,1152]{2,1,0:T(8,128)}, u32[]{:S(2)}, u32[]{:S(2)}) collective-permute-start(f32[2,256,1152]{2,1,0:T(8,128)} %maximum_maximum_fusion.1), channel_id=1, source_target_pairs={{2,0},{4,2},{6,4},{8,6},{10,8},{12,10},{14,12},{16,14},{18,16},{20... | collective-permute-start | bytes 7077896 | tf_op jit(solution)/shard_map/ppermute | solution.py:10
  160.9 59.7 %copy-start.28 = (f32[2,256,512]{2,1,0:T(8,128)S(1)}, f32[2,256,512]{2,1,0:T(8,128)}, u32[]{:S(2)}) copy-start(f32[2,256,512]{2,1,0:T(8,128)} %get-tuple-element.13) | copy-start | bytes 3145732
  160.9 59.7 %copy-start.30 = (f32[2,256,512]{2,1,0:T(8,128)S(1)}, f32[2,256,512]{2,1,0:T(8,128)}, u32[]{:S(2)}) copy-start(f32[2,256,512]{2,1,0:T(8,128)} %copy-done.29) | copy-start | bytes 3145732
  160.9 59.6 %copy-start.34 = (f32[1,2,256,512]{3,2,1,0:T(8,128)S(1)}, f32[1,2,256,512]{3,2,1,0:T(8,128)}, u32[]{:S(2)}) copy-start(f32[1,2,256,512]{3,2,1,0:T(8,128)} %param.7) | copy-start | bytes 3145732
  162.5 58.0 %collective-permute-start.1 = (f32[2,256,1152]{2,1,0:T(8,128)}, f32[2,256,1152]{2,1,0:T(8,128)}, u32[]{:S(2)}, u32[]{:S(2)}) collective-permute-start(f32[2,256,1152]{2,1,0:T(8,128)} %maximum_maximum_fusion), channel_id=1, source_target_pairs={{0,2},{2,4},{4,6},{6,8},{8,10},{10,12},{12,14},{14,16},{16,18},{18... | collective-permute-start | bytes 7077896 | tf_op jit(solution)/shard_map/ppermute | solution.py:10
  224.9 40.1 %all-gather.25.cloned.1.call-start = ((), (), s32[]{:S(2)}) async-start(), calls=%async_computation.5 | async-start | bytes 3145728 | tf_op jit(solution)/shard_map/all_gather | solution.py:25
  238.7 1.6 copy-start.2
  250.2 56.5 %all-gather.27.cloned.1.call-start = ((), (), s32[]{:S(2)}) async-start(), calls=%async_computation.6 | async-start | bytes 3145728 | tf_op jit(solution)/shard_map/all_gather | solution.py:25
  265.0 2.2 copy-start.15
  274.7 2.0 copy-start.35
  275.9 9.5 %copy-start.41 = (f32[1,2,256,128]{3,2,1,0:T(8,128)S(1)}, f32[1,2,256,128]{3,2,1,0:T(8,128)}, u32[]{:S(2)}) copy-start(f32[1,2,256,128]{3,2,1,0:T(8,128)} %param.11) | copy-start | bytes 786436
  275.9 38.5 %all-gather.29.cloned.1.call-start = ((), (), s32[]{:S(2)}) async-start(), calls=%async_computation.7 | async-start | bytes 3145728 | tf_op jit(solution)/shard_map/all_gather | solution.py:30
  276.7 64.1 %all-gather.31.cloned.1.call-start = ((), (), s32[]{:S(2)}) async-start(), calls=%async_computation.8 | async-start | bytes 3145728 | tf_op jit(solution)/shard_map/all_gather | solution.py:31
  276.7 29.0 %collective-permute-start.4 = (f32[2,256,512]{2,1,0:T(8,128)S(1)}, f32[2,256,512]{2,1,0:T(8,128)S(1)}, u32[]{:S(2)}, u32[]{:S(2)}) collective-permute-start(f32[2,256,512]{2,1,0:T(8,128)S(1)} %copy-done.35), channel_id=1, source_target_pairs={{4,0},{6,2},{8,4},{10,6},{12,8},{14,10},{16,12},{18,14},{20,16},{2... | collective-permute-start | bytes 3145736 | tf_op jit(solution)/shard_map/ppermute | solution.py:10
  283.4 45.9 %collective-permute-start.6 = (f32[2,256,512]{2,1,0:T(8,128)}, f32[2,256,512]{2,1,0:T(8,128)}, u32[]{:S(2)}, u32[]{:S(2)}) collective-permute-start(f32[2,256,512]{2,1,0:T(8,128)} %get-tuple-element.8), channel_id=1, source_target_pairs={{0,4},{2,6},{4,8},{6,10},{8,12},{10,14},{12,16},{14,18},{16,20},{1... | collective-permute-start | bytes 3145736 | tf_op jit(solution)/shard_map/ppermute | solution.py:10
  285.4 120.8 %all-gather.33.cloned.1.call-start = ((), (), s32[]{:S(2)}) async-start(), calls=%async_computation.9 | async-start | bytes 3145728 | tf_op jit(solution)/shard_map/all_gather | solution.py:25
  306.7 2.6 copy-start.12
  309.3 3.0 copy-start.33
  314.4 2.6 copy-start.7
  317.0 1.7 copy-start.24
  323.2 36.2 %collective-permute-start.5 = (f32[2,256,640]{2,1,0:T(8,128)}, f32[2,256,640]{2,1,0:T(8,128)}, u32[]{:S(2)}, u32[]{:S(2)}) collective-permute-start(f32[2,256,640]{2,1,0:T(8,128)} %maximum_maximum_fusion.2), channel_id=1, source_target_pairs={{0,4},{2,6},{4,8},{6,10},{8,12},{10,14},{12,16},{14,18},{16,20},{1... | collective-permute-start | bytes 3932168 | tf_op jit(solution)/shard_map/ppermute | solution.py:10
  333.5 5.4 %copy-start.25 = (f32[256,512]{1,0:T(8,128)}, f32[256,512]{1,0:T(8,128)S(1)}, u32[]{:S(2)}) copy-start(f32[256,512]{1,0:T(8,128)S(1)} %convolution_subtract_fusion.5) | copy-start | bytes 1572868
  339.5 3.8 copy-start.26
  340.7 2.6 copy-start.9
  344.4 2.1 copy-start.43
  345.5 38.0 %copy-start.27 = (f32[2,256,512]{2,1,0:T(8,128)S(1)}, f32[2,256,512]{2,1,0:T(8,128)}, u32[]{:S(2)}) copy-start(f32[2,256,512]{2,1,0:T(8,128)} %get-tuple-element.7) | copy-start | bytes 3145732
  347.7 35.8 %collective-permute-start.7 = (f32[2,256,640]{2,1,0:T(8,128)}, f32[2,256,640]{2,1,0:T(8,128)}, u32[]{:S(2)}, u32[]{:S(2)}) collective-permute-start(f32[2,256,640]{2,1,0:T(8,128)} %maximum_maximum_fusion.3), channel_id=1, source_target_pairs={{4,0},{6,2},{8,4},{10,6},{12,8},{14,10},{16,12},{18,14},{20,16},{2... | collective-permute-start | bytes 3932168 | tf_op jit(solution)/shard_map/ppermute | solution.py:10
  386.4 47.9 %all-gather.35.cloned.1.call-start = ((), (), s32[]{:S(2)}) async-start(), calls=%async_computation.10 | async-start | bytes 3145728 | tf_op jit(solution)/shard_map/all_gather | solution.py:25
  408.0 1.6 copy-start.1
  434.4 2.2 copy-start.13
  444.9 17.7 %copy-start.8 = (f32[2,512,512]{2,1,0:T(8,128)S(1)}, f32[2,512,512]{2,1,0:T(8,128)}, u32[]{:S(2)}) copy-start(f32[2,512,512]{2,1,0:T(8,128)} %all-gather.29.cloned.1.call-done) | copy-start | bytes 6291460
  446.7 12.1 %collective-permute-start.9 = (f32[2,256,128]{2,1,0:T(8,128)S(1)}, f32[2,256,128]{2,1,0:T(8,128)S(1)}, u32[]{:S(2)}, u32[]{:S(2)}) collective-permute-start(f32[2,256,128]{2,1,0:T(8,128)S(1)} %pad_maximum_fusion), channel_id=1, source_target_pairs={{4,0},{6,2},{8,4},{10,6},{12,8},{14,10},{16,12},{18,14},{20,16},{2... | collective-permute-start | bytes 786440 | tf_op jit(solution)/shard_map/ppermute | solution.py:10
  453.4 13.8 %collective-permute-start.8 = (f32[2,256,128]{2,1,0:T(8,128)S(1)}, f32[2,256,128]{2,1,0:T(8,128)S(1)}, u32[]{:S(2)}, u32[]{:S(2)}) collective-permute-start(f32[2,256,128]{2,1,0:T(8,128)S(1)} %pad_maximum_fusion), channel_id=1, source_target_pairs={{0,4},{2,6},{4,8},{6,10},{8,12},{10,14},{12,16},{14,18},{16,20},{1... | collective-permute-start | bytes 786440 | tf_op jit(solution)/shard_map/ppermute | solution.py:10
  462.6 7.7 %copy-start.10 = (f32[2,512,512]{2,1,0:T(8,128)S(1)}, f32[2,512,512]{2,1,0:T(8,128)}, u32[]{:S(2)}) copy-start(f32[2,512,512]{2,1,0:T(8,128)} %all-gather.31.cloned.1.call-done) | copy-start | bytes 6291460
  477.1 15.2 %copy-start.6 = (f32[2,512,512]{2,1,0:T(8,128)S(1)}, f32[2,512,512]{2,1,0:T(8,128)}, u32[]{:S(2)}) copy-start(f32[2,512,512]{2,1,0:T(8,128)} %all-gather.19.cloned.1.call-done) | copy-start | bytes 6291460
  478.9 10.1 %collective-permute-start.11 = (f32[2,256,128]{2,1,0:T(8,128)S(1)}, f32[2,256,128]{2,1,0:T(8,128)S(1)}, u32[]{:S(2)}, u32[]{:S(2)}) collective-permute-start(f32[2,256,128]{2,1,0:T(8,128)S(1)} %maximum_select_fusion.1), channel_id=1, source_target_pairs={{2,0},{4,2},{6,4},{8,6},{10,8},{12,10},{14,12},{16,14},{18,16},{20... | collective-permute-start | bytes 786440 | tf_op jit(solution)/shard_map/ppermute | solution.py:10
  483.7 13.3 %collective-permute-start.10 = (f32[2,256,128]{2,1,0:T(8,128)S(1)}, f32[2,256,128]{2,1,0:T(8,128)S(1)}, u32[]{:S(2)}, u32[]{:S(2)}) collective-permute-start(f32[2,256,128]{2,1,0:T(8,128)S(1)} %maximum_select_fusion.1), channel_id=1, source_target_pairs={{0,2},{2,4},{4,6},{6,8},{8,10},{10,12},{12,14},{14,16},{16,18},{18... | collective-permute-start | bytes 786440 | tf_op jit(solution)/shard_map/ppermute | solution.py:10
  492.3 8.1 %copy-start.4 = (f32[2,512,512]{2,1,0:T(8,128)S(1)}, f32[2,512,512]{2,1,0:T(8,128)}, u32[]{:S(2)}) copy-start(f32[2,512,512]{2,1,0:T(8,128)} %all-gather.21.cloned.1.call-done) | copy-start | bytes 6291460
  504.3 2.0 copy-start.20
  (5 other events, 5.0 us)
Sparse Core Ops, SparseCore 0:
  9.0 15.8 all-gather.36
  37.0 14.6 all-gather.14
  62.7 14.6 all-gather.16
  78.8 14.6 all-gather.20
  95.0 14.6 all-gather.18
  225.0 11.8 all-gather.22
  250.3 14.6 all-gather.24
  276.1 14.6 all-gather.26
  292.4 14.7 all-gather.28
  308.6 14.6 all-gather.30
  386.6 19.6 all-gather.32
  419.7 14.6 all-gather.34
where the time goes:
time: 525 us; the launch traced here: 517 us
  waiting for transfers between devices  225 us (43%)
  matrix products  154 us (29%)
  starting transfers between devices  54 us (10%)
  other arithmetic  30.5 us (6%)
  blocking collectives  21.1 us (4%)
  local copies, waits for them, and re-layouts  16.4 us (3%)
  between operations  15.7 us (3%)
    ppermute x12, waiting for transfers between devices, from_behind(): return lax.ppermute(x, axis, pairs)  135 us
    all_gather x8, waiting for transfers between devices, gather_square(): return lax.all_gather(block_rows, 'row', axis=1, tiled=True)  88.7 us
    ppermute x12, starting transfers between devices, from_behind(): return lax.ppermute(x, axis, pairs)  52.2 us
    dot_general x33, matrix products, complex_product(): jnp.dot(left_mat[0], right_mat[1], precision=exact, preferred_element_typ...  43.4 us
    dot_general x33, matrix products, complex_product(): jnp.dot(left_mat[0], right_mat[0], precision=exact, preferred_element_typ...  39.1 us
    dot_general x33, matrix products, complex_product(): jnp.dot(left_mat[1], right_mat[1], precision=exact, preferred_element_typ...  38.1 us
    dot_general x33, matrix products, complex_product(): jnp.dot(left_mat[1], right_mat[0], precision=exact, preferred_element_typ...  33.5 us
    all_gather x5, blocking collectives, gather_solution(): return lax.all_gather(vector_rows, 'row', axis=1, tiled=True)  15.8 us
  transfers between devices with their start and end apart: 24, of which 17 were waited for; matrix products, arithmetic and copies ran while one was open for 18% of the time, Pallas kernels for 0%

commit v1 on v0

v1 whole, which is shorter than its diff:
```python
import functools

import jax
import jax.numpy as jnp
from jax import lax
from jax.experimental import pallas as pl
from jax.experimental.pallas import tpu as pltpu
from jax.sharding import PartitionSpec as P

F32 = jnp.float32
BF16 = jnp.bfloat16
N = 512
H = 256
Q = 128

R_A, R_E, R_L, R_U, R_YCI, R_CC, R_CCP = 0, 1, 2, 3, 4, 5, 6
R_D, R_DP = 7, 9
R_ZW, R_YCO = 11, 12
R_YIN = 13
R_YE = 17
R_ZB, R_SA = 19, 20
R_Z = 21
R_SC, R_FIN = 23, 24
N_RECV = 25
N_SEND = 20


def dot(a, b):
    return jnp.dot(a, b, preferred_element_type=F32)


def halves(x):
    high = x.astype(BF16)
    return high, (x - high.astype(F32)).astype(BF16)


def put_split(dst, rs, cs, re, im):
    for plane, value in enumerate((re, im, re + im)):
        high, low = halves(value)
        dst[plane, 0, rs, cs] = high
        dst[plane, 1, rs, cs] = low


def product3(lhs, rs, rhs, cs):
    parts = []
    for plane in range(3):
        ah, al = lhs[plane, 0, rs, :], lhs[plane, 1, rs, :]
        bh, bl = rhs[plane, 0, :, cs], rhs[plane, 1, :, cs]
        parts.append(dot(ah, bh) + dot(ah, bl) + dot(al, bh))
    return parts[0] - parts[1], parts[2] - parts[0] - parts[1]


def product_stack(lhs, rs, stack_high, stack_low):
    real = dot(lhs[0, 0, rs, :], stack_high) + dot(lhs[0, 0, rs, :], stack_low) + dot(lhs[0, 1, rs, :], stack_high)
    imag = dot(lhs[1, 0, rs, :], stack_high) + dot(lhs[1, 0, rs, :], stack_low) + dot(lhs[1, 1, rs, :], stack_high)
    return real[:, :Q] - imag[:, Q:], real[:, Q:] + imag[:, :Q]


def lane_low(shape):
    return lax.broadcasted_iota(jnp.int32, shape, 1) < Q // 2


def vector_product(lhs, stack_ref, emit):
    high, low = halves(stack_ref[...])
    both = jnp.concatenate([high, low], axis=1)
    for t in range(N // H):
        rs = pl.ds(t * H, H)
        out = []
        for plane in range(2):
            wide = dot(lhs[plane, 0, rs, :], both)
            out.append(wide[:, :Q] + wide[:, Q:] + dot(lhs[plane, 1, rs, :], high))
        turned = pltpu.roll(out[1], Q // 2, 1)
        emit(rs, out[0] + jnp.where(lane_low((H, Q)), -turned, turned))


def split_rows(dst, src, row0, scale_identity):
    @pl.loop(0, H // 32)
    def _(t):
        s0 = pl.multiple_of(t * 32, 32)
        d0 = pl.multiple_of(row0 + s0, 32)
        re, im = src[0, pl.ds(s0, 32), :], src[1, pl.ds(s0, 32), :]
        if scale_identity:
            eye = (
                lax.broadcasted_iota(jnp.int32, (32, N), 0) + d0 == lax.broadcasted_iota(jnp.int32, (32, N), 1)
            ).astype(F32)
            re, im = eye - 0.2 * re, -0.2 * im
        put_split(dst, pl.ds(d0, 32), slice(None), re, im)


def split_columns(dst, src, col0, scale_identity):
    c0 = pl.multiple_of(col0, H)

    @pl.loop(0, N // 32)
    def _(t):
        s0 = pl.multiple_of(t * 32, 32)
        re, im = src[0, pl.ds(s0, 32), :], src[1, pl.ds(s0, 32), :]
        if scale_identity:
            eye = (
                lax.broadcasted_iota(jnp.int32, (32, H), 0) + s0 == lax.broadcasted_iota(jnp.int32, (32, H), 1) + c0
            ).astype(F32)
            re, im = eye - 0.2 * re, -0.2 * im
        put_split(dst, pl.ds(s0, 32), pl.ds(c0, H), re, im)


def squares(lhs):
    @pl.loop(0, 2)
    def _(k):
        src, dst = lhs.at[k], lhs.at[k + 1]

        @pl.loop(0, 4)
        def _(t):
            rs = pl.ds(pl.multiple_of((t // 2) * H, H), H)
            cs = pl.ds(pl.multiple_of((t % 2) * H, H), H)
            re, im = product3(src, rs, src, cs)
            put_split(dst, rs, cs, re, im)


def split_x(xs, x):
    @pl.loop(0, N // 32)
    def _(t):
        rs = pl.ds(pl.multiple_of(t * 32, 32), 32)
        put_split(xs, rs, slice(None), x[0, rs, :], x[1, rs, :])


def apply_series(lhs, x, xs):
    split_x(xs.at[0], x)

    @pl.loop(0, 6)
    def _(u):
        k, t = u // 2, u % 2
        rs = pl.ds(pl.multiple_of(t * H, H), H)
        re, im = product3(lhs.at[k], rs, xs.at[k % 2], slice(None))
        re, im = x[0, rs, :] + re, x[1, rs, :] + im
        x[0, rs, :] = re
        x[1, rs, :] = im
        put_split(xs.at[1 - k % 2], rs, slice(None), re, im)


def kernel(
    slabs,
    a_ref, l_ref, u_ref, tw_ref, e_ref, o_ref,
    onehot, lt, ut, a_oth, l_oth, u_oth, x_ci, x_co, x_w, y_oth, cc_own, cc_oth,
    d_own, d_oth, zw_oth, yco_oth, yin, yein, es, e_send, vec, ye, zb, sa, zin, sc, fin,
    lhs, lc, xs, send_sem, recv_sem,
):
    slab = lax.axis_index("slab")
    r = lax.axis_index("row")
    role = lax.rem(slab, 4)
    odd = lax.rem(role, 2) == 1
    plus = lax.rem(slab + 1, slabs)
    minus = lax.rem(slab + slabs - 1, slabs)
    mine, other = r * H, (1 - r) * H
    mine = pl.multiple_of(mine, H)
    other = pl.multiple_of(other, H)
    partner = (slab, 1 - r)

    barrier = pltpu.get_barrier_semaphore()
    for where in (partner, (plus, r), (minus, r)):
        pl.semaphore_signal(barrier, inc=1, device_id=where, device_id_type=pl.DeviceIdType.MESH)
    pl.semaphore_wait(barrier, 3)

    def copy(src, dst, send, recv, where):
        return pltpu.make_async_remote_copy(
            src_ref=src, dst_ref=dst, send_sem=send_sem.at[send], recv_sem=recv_sem.at[recv],
            device_id=where, device_id_type=pl.DeviceIdType.MESH,
        )

    def arrived(dst, recv):
        copy(dst, dst, 0, recv, partner).wait_recv()

    c_a = copy(a_ref, a_oth, 0, R_A, partner)
    c_a.start()

    def stacked(which):
        er, ei = e_ref[0], e_ref[1]
        low = jnp.where(which == 0, er, pltpu.roll(er, Q // 2, 1))
        high = jnp.where(which == 0, pltpu.roll(ei, Q // 2, 1), ei)
        return jnp.where(lane_low((H, Q)), low, high)

    e_send[...] = stacked(1 - r)
    c_e = copy(e_send, es.at[pl.ds(mine, H), :], 1, R_E, partner)
    c_e.start()
    es[pl.ds(mine, H), :] = stacked(r)

    @pl.loop(0, N // 64)
    def _(t):
        s0 = pl.multiple_of(t * 64, 64)
        hit = lax.broadcasted_iota(jnp.int32, (64, N), 0) + s0 == tw_ref[...]
        onehot[pl.ds(s0, 64), :] = hit.astype(F32).astype(BF16)

    keep_l = (slab > 0).astype(F32)
    keep_u = (slab < slabs - 1).astype(F32)
    for src, dst, keep in ((l_ref, lt, keep_l), (u_ref, ut, keep_u)):
        @pl.loop(0, 2)
        def _(t):
            high, low = halves(src[t])
            dst[t] = (dot(high, onehot[...]) + dot(low, onehot[...])) * keep

    def send_columns(x, dst, base_send, base_recv, where):
        out = []
        for j in range(2):
            view = pl.ds(j * Q, Q)
            c = copy(x.at[:, :, view], dst.at[:, :, view], base_send + j, base_recv + j, where)
            c.start()
            out.append(c)
        return out

    @pl.when(odd)
    def _():
        is_b = role == 1
        inner = (jnp.where(is_b, plus, minus), r)
        outer = (jnp.where(is_b, minus, plus), r)
        side = jnp.where(is_b, 0, 1)
        started = []

        def go(c):
            c.start()
            started.append(c)

        @pl.when(jnp.logical_not(is_b))
        def _():
            @pl.loop(0, H // 8)
            def _(t):
                rs = pl.ds(pl.multiple_of(t * 8, 8), 8)
                for plane in range(2):
                    keep = lt[plane, rs, :]
                    lt[plane, rs, :] = ut[plane, rs, :]
                    ut[plane, rs, :] = keep

        go(copy(ut.at[:, :, pl.ds(other, H)], l_oth.at[:, :, pl.ds(0, H)], 2, R_L, partner))
        go(copy(lt.at[:, :, pl.ds(other, H)], u_oth.at[:, :, pl.ds(0, H)], 3, R_U, partner))
        arrived(a_oth, R_A)
        split_rows(lhs.at[0], a_ref, mine, True)
        split_rows(lhs.at[0], a_oth, other, True)
        squares(lhs)

        def gather_x(x, own, oth):
            for plane in range(2):
                x[plane, pl.ds(mine, H), :] = 0.2 * own[plane, :, pl.ds(mine, H)]
                x[plane, pl.ds(other, H), :] = 0.2 * oth[plane, :, pl.ds(0, H)]

        arrived(l_oth.at[:, :, pl.ds(0, H)], R_L)
        gather_x(x_ci, ut, l_oth)
        apply_series(lhs, x_ci, xs)
        started.extend(send_columns(x_ci, yin.at[side], 4, R_YIN + 2 * side, inner))
        go(copy(x_ci, y_oth, 6, R_YCI, partner))

        arrived(es.at[pl.ds(other, H), :], R_E)
        vec[...] = 0.2 * es[...]
        for k in range(3):
            def emit(rs, value, k=k):
                ye[rs, :] = vec[rs, :] + value
            vector_product(lhs.at[k], vec, emit)
            if k < 2:
                vec[...] = ye[...]
        go(copy(ye, yein.at[side], 7, R_YE + side, inner))

        arrived(u_oth.at[:, :, pl.ds(0, H)], R_U)
        gather_x(x_co, lt, u_oth)
        apply_series(lhs, x_co, xs)
        go(copy(x_co, yco_oth, 8, R_YCO, partner))

        arrived(cc_own, R_CC)
        go(copy(cc_own, cc_oth, 9, R_CCP, partner))
        split_rows(lc.at[0], cc_own, mine, False)
        arrived(y_oth, R_YCI)
        split_columns(lc.at[1], x_ci, mine, False)
        split_columns(lc.at[1], y_oth, other, False)
        arrived(cc_oth, R_CCP)
        split_rows(lc.at[0], cc_oth, other, False)

        @pl.loop(0, 2)
        def _(t):
            rs = pl.ds(pl.multiple_of(t * H, H), H)
            re, im = product3(lc.at[0], rs, xs.at[1], slice(None))
            x_w[0, rs, :] = 0.2 * re
            x_w[1, rs, :] = 0.2 * im

        for j in range(2):
            view = pl.ds(j * Q, Q)
            arrived(d_own.at[:, :, view], R_D + j)
            go(copy(d_own.at[:, :, view], d_oth.at[:, :, view], 10 + j, R_DP + j, partner))
        split_columns(lhs.at[0], d_own, mine, True)
        for j in range(2):
            arrived(d_oth.at[:, :, pl.ds(j * Q, Q)], R_DP + j)
        split_columns(lhs.at[0], d_oth, other, True)
        squares(lhs)
        apply_series(lhs, x_w, xs)
        go(copy(x_w, zw_oth, 12, R_ZW, partner))

        @pl.loop(0, 2)
        def _(t):
            rs = pl.ds(pl.multiple_of(t * H, H), H)
            re, im = product3(lc.at[1], rs, xs.at[1], slice(None))
            yin[0, 0, rs, :] = x_co[0, rs, :] + re
            yin[0, 1, rs, :] = x_co[1, rs, :] + im
        started.extend(send_columns(yin.at[0], yin.at[side], 13, R_YIN + 2 * side, outer))

        arrived(yco_oth, R_YCO)
        split_columns(lc.at[2], x_co, mine, False)
        split_columns(lc.at[2], yco_oth, other, False)
        arrived(zw_oth, R_ZW)
        split_columns(lc.at[0], x_w, mine, False)
        split_columns(lc.at[0], zw_oth, other, False)

        arrived(zb, R_ZB)
        def emit_q(rs, value):
            vec[rs, :] = ye[rs, :] - value
        vector_product(lc.at[1], zb, emit_q)
        go(copy(vec, yein.at[side], 15, R_YE + side, outer))

        arrived(sa, R_SA)
        def emit_z(rs, value):
            es[rs, :] = value
        vector_product(lc.at[0], sa, emit_z)
        go(copy(es, zin.at[side], 16, R_Z + side, inner))
        def emit_w(rs, value):
            yein[0, rs, :] = ye[rs, :] - value
        vector_product(lc.at[2], sa, emit_w)

        arrived(sc, R_SC)
        def emit_s(rs, value):
            zin[0, rs, :] = yein[0, rs, :] - value
        vector_product(lc.at[1], sc, emit_s)
        for c in started:
            c.wait_send()

    @pl.when(jnp.logical_not(odd))
    def _():
        is_c = role == 2
        sides = ((jnp.where(is_c, minus, plus), r), (jnp.where(is_c, plus, minus), r))
        started = []

        def go(c):
            c.start()
            started.append(c)

        go(copy(lt, l_oth, 2, R_L, partner))
        go(copy(ut, u_oth, 3, R_U, partner))

        @pl.when(is_c)
        def _():
            copy(lt, cc_own, 4, R_CC, sides[0]).start()
            copy(ut, cc_own, 5, R_CC, sides[1]).start()

        low = jnp.where(is_c, 0, 1)
        split_rows(lc.at[low], lt, mine, False)
        split_rows(lc.at[1 - low], ut, mine, False)
        arrived(l_oth, R_L)
        split_rows(lc.at[low], l_oth, other, False)
        arrived(u_oth, R_U)
        split_rows(lc.at[1 - low], u_oth, other, False)
        arrived(a_oth, R_A)
        arrived(es.at[pl.ds(other, H), :], R_E)

        for j in range(2):
            view = pl.ds(j * Q, Q)
            column = pl.ds(pl.multiple_of(mine + j * Q, Q), Q)
            stacks = []
            for side in range(2):
                arrived(yin.at[side, :, :, view], R_YIN + 2 * side + j)
                stacks.append(halves(jnp.concatenate([yin[side, 0, :, view], yin[side, 1, :, view]], axis=1)))
            for source, row0 in ((a_ref, mine), (a_oth, other)):
                rs = pl.ds(row0, H)
                re, im = source[0, :, column], source[1, :, column]
                for side in range(2):
                    dre, dim = product_stack(lc.at[side], rs, *stacks[side])
                    re, im = re - dre, im - dim
                d_own[0, rs, view] = re
                d_own[1, rs, view] = im
            go(copy(d_own.at[:, :, view], d_oth.at[:, :, view], 6 + j, R_DP + j, partner))

            @pl.when(is_c)
            def _():
                for side in range(2):
                    copy(
                        d_own.at[:, :, view], d_own.at[:, :, view], 8 + 2 * j + side, R_D + j, sides[side]
                    ).start()

        split_columns(lhs.at[0], d_own, mine, True)
        for j in range(2):
            arrived(d_oth.at[:, :, pl.ds(j * Q, Q)], R_DP + j)
        split_columns(lhs.at[0], d_oth, other, True)
        for side in range(2):
            arrived(yein.at[side], R_YE + side)
            def emit_b(rs, value):
                es[rs, :] = es[rs, :] - value
            vector_product(lc.at[side], yein.at[side], emit_b)
        es[...] = 0.2 * es[...]
        zb[...] = es[...]

        @pl.loop(0, 7)
        def _(step):
            def emit_h(rs, value):
                vec[rs, :] = es[rs, :] + value
            vector_product(lhs.at[0], zb, emit_h)
            zb[...] = vec[...]

        @pl.when(is_c)
        def _():
            first = [copy(zb, zb, 12 + side, R_ZB, sides[side]) for side in range(2)]
            for c in first:
                c.start()
            for side in range(2):
                arrived(zin.at[side], R_Z + side)
            sc[...] = zb[...] + zin[0] + zin[1]
            second = [copy(sc, sc, 14 + side, R_SC, sides[side]) for side in range(2)]
            for c in second:
                c.start()
            copy(lt, cc_own, 4, R_CC, sides[0]).wait_send()
            copy(ut, cc_own, 5, R_CC, sides[1]).wait_send()
            for j in range(2):
                view = pl.ds(j * Q, Q)
                for side in range(2):
                    copy(
                        d_own.at[:, :, view], d_own.at[:, :, view], 8 + 2 * j + side, R_D + j, sides[side]
                    ).wait_send()
            for c in first + second:
                c.wait_send()
            zin[0] = sc[...]

        @pl.when(jnp.logical_not(is_c))
        def _():
            both = [copy(zb, sa, 12 + side, R_SA, sides[side]) for side in range(2)]
            for c in both:
                c.start()
            zin[0] = zb[...]
            for c in both:
                c.wait_send()

        for c in started:
            c.wait_send()

    result = zin.at[0]
    c_f = copy(result.at[pl.ds(other, H), :], fin, 17, R_FIN, partner)
    c_f.start()
    own = result[pl.ds(mine, H), :]
    arrived(fin, R_FIN)
    oth = fin[...]
    first = jnp.where(r == 0, own, oth)
    second = jnp.where(r == 0, oth, own)
    low = lane_low((H, Q))
    o_ref[0] = jnp.where(low, first, pltpu.roll(second, Q // 2, 1))
    o_ref[1] = jnp.where(low, pltpu.roll(first, Q // 2, 1), second)
    c_f.wait_send()
    c_a.wait_send()
    c_e.wait_send()


def solution(mesh):
    slabs = mesh.shape["slab"]

    def body(diag_block, lower_block, upper_block, twist, excitation):
        vmem = pl.BlockSpec(memory_space=pltpu.VMEM)
        rows = pltpu.VMEM((2, H, N), F32)
        columns = pltpu.VMEM((2, N, H), F32)
        vector = pltpu.VMEM((N, Q), F32)
        out = pl.pallas_call(
            functools.partial(kernel, slabs),
            out_shape=jax.ShapeDtypeStruct((2, H, Q), F32),
            in_specs=[vmem] * 5,
            out_specs=vmem,
            scratch_shapes=[
                pltpu.VMEM((N, N), BF16),
                rows, rows,
                rows, rows, rows,
                columns, columns, columns, columns,
                rows, rows,
                columns, columns, columns, columns,
                pltpu.VMEM((2, 2, N, H), F32),
                pltpu.VMEM((2, N, Q), F32),
                vector, pltpu.VMEM((H, Q), F32),
                vector, vector, vector, vector,
                pltpu.VMEM((2, N, Q), F32),
                vector, pltpu.VMEM((H, Q), F32),
                pltpu.VMEM((3, 3, 2, N, N), BF16),
                pltpu.VMEM((3, 3, 2, N, N), BF16),
                pltpu.VMEM((2, 3, 2, N, H), BF16),
                pltpu.SemaphoreType.DMA((N_SEND,)),
                pltpu.SemaphoreType.DMA((N_RECV,)),
            ],
            compiler_params=pltpu.CompilerParams(
                collective_id=0, has_side_effects=True, vmem_limit_bytes=60 * 1024 * 1024
            ),
        )(diag_block[0], lower_block[0], upper_block[0], twist, excitation[0])
        return out[None]

    return jax.shard_map(
        body,
        mesh=mesh,
        in_specs=(
            P("slab", None, "row", None),
            P("slab", None, "row", None),
            P("slab", None, "row", None),
            P("slab", None),
            P("slab", None, "row", None),
        ),
        out_specs=P("slab", None, "row", None),
        check_vma=False,
    )
```

time: 525 us -> 144 us (0.27)
  the two profiles are of different devices: /device:TPU:33 before, /device:TPU:3 now
where the time goes in v1:
time: 144 us
  Pallas kernels  142 us (99%)
  local copies, waits for them, and re-layouts  1.67 us (1%)
    pallas_call x1, Pallas kernels, body(): pl.pallas_call(functools.partial(kernel, slabs), out_shape=jax.ShapeDtype...  142 us

profile of v1, /device:TPU:3, one launch (start us, length us, event | category | flops | bytes accessed | tf_op | source)
XLA Modules:
  0.0 143.8 jit_solution(8851096131723816298)
XLA Ops:
  0.0 142.1 %shard_map.55 = f32[2,256,128]{2,1,0:T(8,128)} custom-call(f32[2,256,512]{2,1,0:T(8,128)} %bitcast.5, f32[2,256,512]{2,1,0:T(8,128)} %bitcast.6, f32[2,256,512]{2,1,0:T(8,128)} %bitcast.7, s32[1,512]{1,0:T(1,128)} %tw_ref.1, f32[2,256,128]{2,1,0:T(8,128)} %bitcast.9), custom_call_target="tpu_custom_call" | custom-call | tf_op jit(solution)/shard_map/pallas_call | solution.py:458
  142.1 1.7 %copy.7 = f32[1,2,256,128]{3,2,1,0:T(8,128)} copy(f32[1,2,256,128]{3,2,1,0:T(8,128)} %bitcast.8) | data formatting | bytes 524288

commit v2 on v0

v2 whole, which is shorter than its diff:
```python
import functools

import jax
import jax.numpy as jnp
from jax import lax
from jax.experimental import pallas as pl
from jax.experimental.pallas import tpu as pltpu
from jax.sharding import PartitionSpec as P

F32 = jnp.float32
BF16 = jnp.bfloat16
N = 512
H = 256
Q = 128
C = 4
K = 4

R_A, R_E, R_T, R_CI, R_CO, R_CC, R_CCP, R_FIN, R_ZB = 0, 1, 2, 4, 5, 6, 7, 8, 9
R_YE = 10
R_YCI, R_D, R_DP, R_P, R_R, R_ZWX = 12, 16, 20, 24, 28, 32
R_YIN, R_ZW, R_ZWP, R_S = 36, 44, 52, 60
N_RECV = 68
N_SEND = 64


def dot(a, b):
    return jnp.dot(a, b, preferred_element_type=F32)


def halves(x):
    high = x.astype(BF16)
    return high, (x - high.astype(F32)).astype(BF16)


def put_split(dst, rs, cs, re, im, planes):
    for plane, value in enumerate((re, im, re + im)[:planes]):
        high, low = halves(value)
        dst[plane, 0, rs, cs] = high
        dst[plane, 1, rs, cs] = low


def product3(lhs, rs, rhs, cs):
    parts = []
    for plane in range(3):
        ah, al = lhs[plane, 0, rs, :], lhs[plane, 1, rs, :]
        bh, bl = rhs[plane, 0, :, cs], rhs[plane, 1, :, cs]
        parts.append(dot(ah, bh) + dot(ah, bl) + dot(al, bh))
    return parts[0] - parts[1], parts[2] - parts[0] - parts[1]


def lane_low(shape):
    return lax.broadcasted_iota(jnp.int32, shape, 1) < Q // 2


def turn(x):
    return pltpu.roll(x, Q // 2, 1)


def pack(re, im):
    low = lane_low(re.shape)
    return jnp.where(low, re, turn(im)), jnp.where(low, turn(re), im)


def unpack(first, second):
    low = lane_low(first.shape)
    return jnp.where(low, first, turn(second)), jnp.where(low, turn(first), second)


def vector_product(lhs, stack_ref, emit):
    high, low = halves(stack_ref[...])
    both = jnp.concatenate([high, low], axis=1)
    for t in range(N // H):
        rs = pl.ds(t * H, H)
        out = []
        for plane in range(2):
            wide = dot(lhs[plane, 0, rs, :], both)
            out.append(wide[:, :Q] + wide[:, Q:] + dot(lhs[plane, 1, rs, :], high))
        turned = turn(out[1])
        emit(rs, out[0] + jnp.where(lane_low((H, Q)), -turned, turned))


def put(dst, lhs, src, base=None, scale=1.0):
    def emit(rs, value):
        value = value if scale == 1.0 else scale * value
        dst[rs, :] = value if base is None else base[rs, :] + value

    vector_product(lhs, src, emit)


def identity_minus(re, im, row0, col0):
    eye = (
        lax.broadcasted_iota(jnp.int32, re.shape, 0) + row0 == lax.broadcasted_iota(jnp.int32, re.shape, 1) + col0
    ).astype(F32)
    return eye - 0.2 * re, -0.2 * im


def split_rows(dst, src, row0, inverse, planes):
    @pl.loop(0, H // 32)
    def _(t):
        s0 = pl.multiple_of(t * 32, 32)
        d0 = pl.multiple_of(row0 + s0, 32)
        re, im = src[0, pl.ds(s0, 32), :], src[1, pl.ds(s0, 32), :]
        if inverse:
            re, im = identity_minus(re, im, d0, 0)
        put_split(dst, pl.ds(d0, 32), slice(None), re, im, planes)


def split_chunks(dst, src, col0, inverse, planes):
    @pl.loop(0, N // 32)
    def _(t):
        rs = pl.ds(pl.multiple_of(t * 32, 32), 32)
        for m in range(C // 2):
            c0 = pl.multiple_of(col0 + m * Q, Q)
            re, im = unpack(src[2 * m, rs, :], src[2 * m + 1, rs, :])
            if inverse:
                re, im = identity_minus(re, im, t * 32, c0)
            put_split(dst, rs, pl.ds(c0, Q), re, im, planes)


def stack_rows(dst, dst_row0, src, col0, scale):
    @pl.loop(0, H // 32)
    def _(t):
        rs = pl.ds(pl.multiple_of(t * 32, 32), 32)
        ds = pl.ds(pl.multiple_of(dst_row0 + t * 32, 32), 32)
        for m in range(C // 2):
            cs = pl.ds(pl.multiple_of(col0 + m * Q, Q), Q)
            first, second = pack(src[0, rs, cs], src[1, rs, cs])
            dst[2 * m, ds, :] = scale * first
            dst[2 * m + 1, ds, :] = scale * second


def square(src, dst, planes):
    @pl.loop(0, 4)
    def _(t):
        rs = pl.ds(pl.multiple_of((t // 2) * H, H), H)
        cs = pl.ds(pl.multiple_of((t % 2) * H, H), H)
        re, im = product3(src, rs, src, cs)
        put_split(dst, rs, cs, re, im, planes)


def series(lhs, x, va, vb, fourth):
    put(va, lhs.at[0], x, x)
    put(vb, lhs.at[1], va, va)
    if fourth:
        put(x, lhs.at[2], vb, vb)
    else:
        put(va, lhs.at[1], vb)
        put(x, lhs.at[1], va, vb)


def kernel(
    slabs,
    a_ref, l_ref, u_ref, tw_ref, e_ref, o_ref,
    onehot, tw, a_oth, tw_oth, a_st, st_send, x_ci, x_co, x_w, y_oth, cc_own, cc_oth,
    d_own, d_oth, p_own, p_oth, zwx, r_own, r_oth, yin, zwo, yein, es, e_send,
    va, vb, ye, zb, qv, res, sin, fin, lhs, lc, send_sem, recv_sem,
):
    slab = lax.axis_index("slab")
    r = lax.axis_index("row")
    role = lax.rem(slab, 4)
    odd = lax.rem(role, 2) == 1

    def slab_at(offset):
        return lax.rem(slab + slabs + offset, slabs)

    plus, minus = slab_at(1), slab_at(-1)
    mine = pl.multiple_of(r * H, H)
    other = pl.multiple_of((1 - r) * H, H)
    partner = (slab, 1 - r)

    barrier = pltpu.get_barrier_semaphore()
    for where in (partner, (plus, r), (minus, r), (slab_at(4), r), (slab_at(-4), r)):
        pl.semaphore_signal(barrier, inc=1, device_id=where, device_id_type=pl.DeviceIdType.MESH)
    pl.semaphore_wait(barrier, 5)

    def copy(src, dst, send, recv, where):
        return pltpu.make_async_remote_copy(
            src_ref=src, dst_ref=dst, send_sem=send_sem.at[send], recv_sem=recv_sem.at[recv],
            device_id=where, device_id_type=pl.DeviceIdType.MESH,
        )

    def arrived(dst, recv):
        copy(dst, dst, 0, recv, partner).wait_recv()

    c_a = copy(a_ref, a_oth, 0, R_A, partner)
    c_a.start()

    def stacked(which):
        first, second = pack(e_ref[0], e_ref[1])
        return jnp.where(which == 0, first, second)

    e_send[...] = stacked(1 - r)
    c_e = copy(e_send, es.at[pl.ds(mine, H), :], 1, R_E, partner)
    c_e.start()
    es[pl.ds(mine, H), :] = stacked(r)

    @pl.loop(0, N // 64)
    def _(t):
        s0 = pl.multiple_of(t * 64, 64)
        hit = lax.broadcasted_iota(jnp.int32, (64, N), 0) + s0 == tw_ref[...]
        onehot[pl.ds(s0, 64), :] = hit.astype(F32).astype(BF16)

    place_l = 1 - role // 2
    keep_l = (slab > 0).astype(F32)
    keep_u = (slab < slabs - 1).astype(F32)
    for src, place, keep in ((l_ref, place_l, keep_l), (u_ref, 1 - place_l, keep_u)):
        @pl.loop(0, 2)
        def _(t):
            high, low = halves(src[t])
            tw[place, t] = (dot(high, onehot[...]) + dot(low, onehot[...])) * keep

    def sender(first):
        count = [first]
        pending = []

        def prepare(make, n=1):
            base = count[0]
            count[0] += n
            assert count[0] <= N_SEND
            pending.append((make, base, n))
            return lambda j=0: make(j, base + j).start()

        def finish():
            for make, base, n in pending:
                for j in range(n):
                    make(j, base + j).wait_send()

        return prepare, finish

    @pl.when(odd)
    def _():
        is_b = role == 1
        inner = (jnp.where(is_b, plus, minus), r)
        outer = (jnp.where(is_b, minus, plus), r)
        sibling = (jnp.where(is_b, slab_at(-4), slab_at(4)), r)
        side = jnp.where(is_b, 0, 1)
        prepare, finish = sender(2)

        s_ci = prepare(lambda j, s: copy(st_send.at[0], x_ci.at[:, pl.ds(mine, H), :], s, R_CI, partner))
        s_co = prepare(lambda j, s: copy(st_send.at[1], x_co.at[:, pl.ds(mine, H), :], s, R_CO, partner))
        s_yci = prepare(lambda j, s: copy(x_ci.at[j], yin.at[side, j], s, R_YIN + 4 * side + j, inner), C)
        s_ycip = prepare(lambda j, s: copy(x_ci.at[j], y_oth.at[j], s, R_YCI + j, partner), C)
        s_ye = prepare(lambda j, s: copy(ye, yein.at[side], s, R_YE + side, inner))
        s_cc = prepare(lambda j, s: copy(cc_own, cc_oth, s, R_CCP, partner))
        s_d = prepare(lambda j, s: copy(d_own.at[j], d_oth.at[j], s, R_DP + j, partner), C)
        s_p = prepare(lambda j, s: copy(p_own.at[j], yin.at[side, j], s, R_YIN + 4 * side + j, outer), C)
        s_pp = prepare(lambda j, s: copy(p_own.at[j], p_oth.at[j], s, R_P + j, partner), C)
        s_zw = prepare(lambda j, s: copy(x_w.at[j], yin.at[side, j], s, R_ZW + 4 * side + j, inner), C)
        s_q = prepare(lambda j, s: copy(qv, yein.at[side], s, R_YE + side, outer))
        s_r = prepare(lambda j, s: copy(r_own.at[j], r_oth.at[j], s, R_R + j, partner), C)

        def piece(ref, j):
            return ref.at[pl.ds(j * Q, Q), :]

        s_in = prepare(lambda j, s: copy(piece(sin.at[0], j), piece(sin.at[side], j), s, R_S + 4 * side + j, inner), K)
        s_sib = prepare(lambda j, s: copy(piece(sin.at[0], j), piece(sin.at[1], j), s, R_S + 4 + j, sibling), K)

        stack_rows(st_send.at[0], 0, tw.at[0], other, 0.2)
        s_ci()
        stack_rows(x_ci, mine, tw.at[0], mine, 0.2)
        arrived(a_oth, R_A)
        split_rows(lhs.at[0], a_ref, mine, True, 3)
        split_rows(lhs.at[0], a_oth, other, True, 3)
        square(lhs.at[0], lhs.at[1], 3)
        arrived(x_ci.at[:, pl.ds(other, H), :], R_CI)
        series(lhs, x_ci.at[0], va, vb, False)
        s_yci(0)
        s_ycip(0)
        square(lhs.at[1], lhs.at[2], 2)

        @pl.loop(1, C)
        def _(j):
            series(lhs, x_ci.at[j], va, vb, True)
            s_yci(j)
            s_ycip(j)

        stack_rows(st_send.at[1], 0, tw.at[1], other, 0.2)
        s_co()
        stack_rows(x_co, mine, tw.at[1], mine, 0.2)
        arrived(es.at[pl.ds(other, H), :], R_E)
        ye[...] = 0.2 * es[...]
        series(lhs, ye, va, vb, True)
        s_ye()
        arrived(x_co.at[:, pl.ds(other, H), :], R_CO)

        @pl.loop(0, C)
        def _(j):
            series(lhs, x_co.at[j], va, vb, True)

        arrived(cc_own, R_CC)
        s_cc()
        split_rows(lc.at[0], cc_own, mine, False, 2)
        split_chunks(lc.at[1], x_ci, mine, False, 2)
        for j in range(C):
            arrived(y_oth.at[j], R_YCI + j)
        split_chunks(lc.at[1], y_oth, other, False, 2)
        arrived(cc_oth, R_CCP)
        split_rows(lc.at[0], cc_oth, other, False, 2)

        @pl.loop(0, C)
        def _(j):
            put(x_w.at[j], lc.at[0], x_co.at[j], scale=0.2)

        for j in range(C):
            arrived(d_own.at[j], R_D + j)
            s_d(j)
        split_chunks(lhs.at[0], d_own, mine, True, 3)
        for j in range(C):
            arrived(d_oth.at[j], R_DP + j)
        split_chunks(lhs.at[0], d_oth, other, True, 3)
        square(lhs.at[0], lhs.at[1], 3)

        def reduced(j, fourth):
            series(lhs, x_w.at[j], va, vb, fourth)
            s_zw(j)
            put(p_own.at[j], lc.at[1], x_w.at[j], x_co.at[j])
            s_p(j)
            s_pp(j)

        reduced(0, False)
        square(lhs.at[1], lhs.at[2], 2)

        @pl.loop(1, C)
        def _(j):
            reduced(j, True)

        arrived(zb, R_ZB)
        put(qv, lc.at[1], zb, ye, -1.0)
        s_q()
        split_chunks(lc.at[2], p_own, mine, False, 2)
        for j in range(C):
            arrived(p_oth.at[j], R_P + j)
        split_chunks(lc.at[2], p_oth, other, False, 2)

        @pl.loop(0, C)
        def _(j):
            arrived(zwx.at[j], R_ZWX + j)
            put(r_own.at[j], lc.at[1], zwx.at[j])
            s_r(j)

        split_chunks(lc.at[0], r_own, mine, False, 2)
        for j in range(C):
            arrived(r_oth.at[j], R_R + j)
        split_chunks(lc.at[0], r_oth, other, False, 2)

        for j in range(K):
            arrived(piece(sin.at[0], j), R_S + j)
            s_in(j)
            s_sib(j)
        put(va, lc.at[2], sin.at[0], qv, -1.0)
        for j in range(K):
            arrived(piece(sin.at[1], j), R_S + 4 + j)
        put(res, lc.at[0], sin.at[1], va, -1.0)
        finish()

    @pl.when(jnp.logical_not(odd))
    def _():
        is_c = role == 2
        sides = ((jnp.where(is_c, minus, plus), r), (jnp.where(is_c, plus, minus), r))
        prepare, finish = sender(2)
        prepare_c, finish_c = sender(24)
        prepare_a, finish_a = sender(24)

        def piece(ref, j):
            return ref.at[pl.ds(j * Q, Q), :]

        s_t = prepare(lambda j, s: copy(tw.at[j], tw_oth.at[j], s, R_T + j, partner), 2)
        s_d = prepare(lambda j, s: copy(d_own.at[j], d_oth.at[j], s, R_DP + j, partner), C)
        s_cc = [prepare_c(lambda j, s, i=i: copy(tw.at[i], cc_own, s, R_CC, sides[i])) for i in range(2)]
        s_dc = [prepare_c(lambda j, s, i=i: copy(d_own.at[j], d_own.at[j], s, R_D + j, sides[i]), C) for i in range(2)]
        s_zb = [prepare_c(lambda j, s, i=i: copy(zb, zb, s, R_ZB, sides[i])) for i in range(2)]
        s_zwp = [
            prepare_c(lambda j, s, i=i: copy(yin.at[i, j], zwo.at[i, j], s, R_ZWP + 4 * i + j, partner), C)
            for i in range(2)
        ]
        s_zwx = [
            prepare_c(lambda j, s, i=i: copy(yin.at[i, j], zwx.at[j], s, R_ZWX + j, sides[1 - i]), C) for i in range(2)
        ]
        s_sa = [
            prepare_a(lambda j, s, i=i: copy(piece(zb, j), piece(sin.at[0], j), s, R_S + j, sides[i]), K)
            for i in range(2)
        ]

        for i in range(2):
            s_t(i)

            @pl.when(is_c)
            def _():
                s_cc[i]()

            split_rows(lc.at[i], tw.at[i], mine, False, 2)
        stack_rows(a_st, mine, a_ref, mine, 1.0)
        arrived(a_oth, R_A)
        stack_rows(a_st, other, a_oth, mine, 1.0)
        for i in range(2):
            arrived(tw_oth.at[i], R_T + i)
            split_rows(lc.at[i], tw_oth.at[i], other, False, 2)
        arrived(es.at[pl.ds(other, H), :], R_E)

        @pl.loop(0, C)
        def _(j):
            arrived(yin.at[0, j], R_YIN + j)
            put(d_own.at[j], lc.at[0], yin.at[0, j], a_st.at[j], -1.0)
            arrived(yin.at[1, j], R_YIN + 4 + j)
            put(d_own.at[j], lc.at[1], yin.at[1, j], d_own.at[j], -1.0)

            @pl.when(is_c)
            def _():
                for i in range(2):
                    s_dc[i](j)

            s_d(j)

        split_chunks(lhs.at[0], d_own, mine, True, 3)
        for j in range(C):
            arrived(d_oth.at[j], R_DP + j)
        split_chunks(lhs.at[0], d_oth, other, True, 3)
        square(lhs.at[0], lhs.at[1], 2)
        for i in range(2):
            arrived(yein.at[i], R_YE + i)
            put(es, lc.at[i], yein.at[i], es, -1.0)
        zb[...] = 0.2 * es[...]
        series(lhs, zb, va, vb, False)

        @pl.when(is_c)
        def _():
            for i in range(2):
                s_zb[i]()

            @pl.loop(0, C)
            def _(j):
                for i in range(2):
                    arrived(yin.at[i, j], R_ZW + 4 * i + j)
                    s_zwx[i](j)
                    s_zwp[i](j)

            for i in range(2):
                split_chunks(lc.at[i], yin.at[i], mine, False, 2)
            for i in range(2):
                for j in range(C):
                    arrived(zwo.at[i, j], R_ZWP + 4 * i + j)
                split_chunks(lc.at[i], zwo.at[i], other, False, 2)
            for i in range(2):
                for j in range(K):
                    arrived(piece(sin.at[i], j), R_S + 4 * i + j)
                put(res, lc.at[i], sin.at[i], zb if i == 0 else res)
            finish_c()

        @pl.when(jnp.logical_not(is_c))
        def _():
            for j in range(K):
                for i in range(2):
                    s_sa[i](j)
            res[...] = zb[...]
            finish_a()

        finish()

    c_f = copy(res.at[pl.ds(other, H), :], fin, N_SEND, R_FIN, partner)
    c_f.start()
    own = res[pl.ds(mine, H), :]
    arrived(fin, R_FIN)
    oth = fin[...]
    re, im = unpack(jnp.where(r == 0, own, oth), jnp.where(r == 0, oth, own))
    o_ref[0] = re
    o_ref[1] = im
    c_f.wait_send()
    c_a.wait_send()
    c_e.wait_send()


def solution(mesh):
    slabs = mesh.shape["slab"]

    def body(diag_block, lower_block, upper_block, twist, excitation):
        vmem = pl.BlockSpec(memory_space=pltpu.VMEM)

        def f32(*shape):
            return pltpu.VMEM(shape, F32)

        rows, chunks, vector = f32(2, H, N), f32(C, N, Q), f32(N, Q)
        out = pl.pallas_call(
            functools.partial(kernel, slabs),
            out_shape=jax.ShapeDtypeStruct((2, H, Q), F32),
            in_specs=[vmem] * 5,
            out_specs=vmem,
            scratch_shapes=[
                pltpu.VMEM((N, N), BF16),
                f32(2, 2, H, N), rows, f32(2, 2, H, N),
                chunks, f32(2, C, H, Q),
                chunks, chunks, chunks, chunks,
                rows, rows,
                chunks, chunks, chunks, chunks,
                chunks, chunks, chunks,
                f32(2, C, N, Q), f32(2, C, N, Q), f32(2, N, Q),
                vector, f32(H, Q),
                vector, vector, vector, vector, vector, vector,
                f32(2, N, Q), f32(H, Q),
                pltpu.VMEM((3, 3, 2, N, N), BF16),
                pltpu.VMEM((3, 2, 2, N, N), BF16),
                pltpu.SemaphoreType.DMA((N_SEND + 1,)),
                pltpu.SemaphoreType.DMA((N_RECV,)),
            ],
            compiler_params=pltpu.CompilerParams(
                collective_id=0, has_side_effects=True, vmem_limit_bytes=60 * 1024 * 1024
            ),
        )(diag_block[0], lower_block[0], upper_block[0], twist, excitation[0])
        return out[None]

    spec = P("slab", None, "row", None)
    return jax.shard_map(
        body,
        mesh=mesh,
        in_specs=(spec, spec, spec, P("slab", None), spec),
        out_specs=spec,
        check_vma=False,
    )
```

time: 525 us -> 128 us (0.24)
  the two profiles are of different devices: /device:TPU:33 before, /device:TPU:7 now
where the time goes in v2:
time: 128 us
  Pallas kernels  126 us (98%)
  local copies, waits for them, and re-layouts  1.67 us (1%)
    pallas_call x1, Pallas kernels, body(): pl.pallas_call(functools.partial(kernel, slabs), out_shape=jax.ShapeDtype...  126 us

profile of v2, /device:TPU:7, one launch (start us, length us, event | category | flops | bytes accessed | tf_op | source)
XLA Modules:
  0.0 127.5 jit_solution(3477218276571145219)
XLA Ops:
  0.0 125.8 %shard_map.55 = f32[2,256,128]{2,1,0:T(8,128)} custom-call(f32[2,256,512]{2,1,0:T(8,128)} %bitcast.5, f32[2,256,512]{2,1,0:T(8,128)} %bitcast.6, f32[2,256,512]{2,1,0:T(8,128)} %bitcast.7, s32[1,512]{1,0:T(1,128)} %tw_ref.1, f32[2,256,128]{2,1,0:T(8,128)} %bitcast.9), custom_call_target="tpu_custom_call" | custom-call | tf_op jit(solution)/shard_map/pallas_call | solution.py:482
  125.9 1.7 %copy.7 = f32[1,2,256,128]{3,2,1,0:T(8,128)} copy(f32[1,2,256,128]{3,2,1,0:T(8,128)} %bitcast.8) | data formatting | bytes 524288

commit v3 on v2

--- a/solution.py
+++ b/solution.py
@@ -19,7 +19,8 @@
 R_YE = 10
 R_YCI, R_D, R_DP, R_P, R_R, R_ZWX = 12, 16, 20, 24, 28, 32
 R_YIN, R_ZW, R_ZWP, R_S = 36, 44, 52, 60
-N_RECV = 68
+R_CT = 68
+N_RECV = 69
 N_SEND = 64
 
 
@@ -151,27 +152,48 @@
 def kernel(
     slabs,
     a_ref, l_ref, u_ref, tw_ref, e_ref, o_ref,
-    onehot, tw, a_oth, tw_oth, a_st, st_send, x_ci, x_co, x_w, y_oth, cc_own, cc_oth,
+    a_own, l_own, u_own, e_own, t_own, t_oth, onehot, tw, a_oth, tw_oth, a_st, st_send, x_ci, x_co, x_w, y_oth, cc_own, cc_oth,
     d_own, d_oth, p_own, p_oth, zwx, r_own, r_oth, yin, zwo, yein, es, e_send,
-    va, vb, ye, zb, qv, res, sin, fin, lhs, lc, send_sem, recv_sem,
+    va, vb, ye, zb, qv, res, sin, fin, lhs, lc, send_sem, recv_sem, load_sem,
 ):
     slab = lax.axis_index("slab")
     r = lax.axis_index("row")
     role = lax.rem(slab, 4)
     odd = lax.rem(role, 2) == 1
 
+    loads = []
+    for k, (src, dst) in enumerate(((a_ref, a_own), (tw_ref, t_own), (l_ref, l_own), (u_ref, u_own), (e_ref, e_own))):
+        load = pltpu.make_async_copy(src, dst, load_sem.at[k])
+        load.start()
+        loads.append(load)
+
     def slab_at(offset):
         return lax.rem(slab + slabs + offset, slabs)
 
     plus, minus = slab_at(1), slab_at(-1)
+    has_plus, has_minus = slab < slabs - 1, slab > 0
     mine = pl.multiple_of(r * H, H)
     other = pl.multiple_of((1 - r) * H, H)
     partner = (slab, 1 - r)
 
     barrier = pltpu.get_barrier_semaphore()
-    for where in (partner, (plus, r), (minus, r), (slab_at(4), r), (slab_at(-4), r)):
-        pl.semaphore_signal(barrier, inc=1, device_id=where, device_id_type=pl.DeviceIdType.MESH)
-    pl.semaphore_wait(barrier, 5)
+    everyone = (
+        (slab >= 0, partner),
+        (has_plus, (plus, r)),
+        (has_minus, (minus, r)),
+        (jnp.logical_and(odd, slab >= 4), (slab_at(-4), r)),
+        (jnp.logical_and(odd, slab < slabs - 4), (slab_at(4), r)),
+        (slab == 0, (slab_at(3), r)),
+        (slab == 3, (slab_at(-3), r)),
+    )
+    total = 0
+    for there, where in everyone:
+        @pl.when(there)
+        def _():
+            pl.semaphore_signal(barrier, inc=1, device_id=where, device_id_type=pl.DeviceIdType.MESH)
+
+        total = total + there.astype(jnp.int32)
+    pl.semaphore_wait(barrier, total)
 
     def copy(src, dst, send, recv, where):
         return pltpu.make_async_remote_copy(
@@ -184,9 +206,21 @@
 
     c_a = copy(a_ref, a_oth, 0, R_A, partner)
     c_a.start()
+    couplings = []
+    for i, (src, where) in enumerate(((l_ref, (minus, r)), (u_ref, (plus, r)))):
+        couplings.append(copy(tw_ref, t_oth, N_SEND + 1 + 2 * i, R_CT, where))
+        couplings.append(copy(src, cc_own, N_SEND + 2 + 2 * i, R_CC, where))
+
+    @pl.when(role == 2)
+    def _():
+        for c in couplings:
+            c.start()
+
+    for load in loads:
+        load.wait()
 
     def stacked(which):
-        first, second = pack(e_ref[0], e_ref[1])
+        first, second = pack(e_own[0], e_own[1])
         return jnp.where(which == 0, first, second)
 
     e_send[...] = stacked(1 - r)
@@ -194,36 +228,60 @@
     c_e.start()
     es[pl.ds(mine, H), :] = stacked(r)
 
-    @pl.loop(0, N // 64)
-    def _(t):
-        s0 = pl.multiple_of(t * 64, 64)
-        hit = lax.broadcasted_iota(jnp.int32, (64, N), 0) + s0 == tw_ref[...]
-        onehot[pl.ds(s0, 64), :] = hit.astype(F32).astype(BF16)
+    def choose(order):
+        @pl.loop(0, N // 64)
+        def _(t):
+            s0 = pl.multiple_of(t * 64, 64)
+            hit = lax.broadcasted_iota(jnp.int32, (64, N), 0) + s0 == order[...]
+            onehot[pl.ds(s0, 64), :] = hit.astype(F32).astype(BF16)
+
+    choose(t_own)
 
     place_l = 1 - role // 2
     keep_l = (slab > 0).astype(F32)
     keep_u = (slab < slabs - 1).astype(F32)
-    for src, place, keep in ((l_ref, place_l, keep_l), (u_ref, 1 - place_l, keep_u)):
+    for src, place, keep in ((l_own, place_l, keep_l), (u_own, 1 - place_l, keep_u)):
         @pl.loop(0, 2)
         def _(t):
             high, low = halves(src[t])
             tw[place, t] = (dot(high, onehot[...]) + dot(low, onehot[...])) * keep
 
+    def twist_rows(dst, src, row0):
+        rs = pl.ds(row0, H)
+
+        @pl.loop(0, 2)
+        def _(t):
+            for part, value in enumerate(halves(src[t])):
+                dst[t, part, rs, :] = dot(value, onehot[...]).astype(BF16)
+
     def sender(first):
         count = [first]
         pending = []
 
-        def prepare(make, n=1):
+        def prepare(make, n=1, when=None):
             base = count[0]
             count[0] += n
             assert count[0] <= N_SEND
-            pending.append((make, base, n))
-            return lambda j=0: make(j, base + j).start()
+            pending.append((make, base, n, when))
+
+            def start(j=0):
+                if when is None:
+                    make(j, base + j).start()
+                else:
+                    pl.when(when)(lambda: make(j, base + j).start())
+
+            return start
 
         def finish():
-            for make, base, n in pending:
-                for j in range(n):
-                    make(j, base + j).wait_send()
+            for make, base, n, when in pending:
+                def wait(make=make, base=base, n=n):
+                    for j in range(n):
+                        make(j, base + j).wait_send()
+
+                if when is None:
+                    wait()
+                else:
+                    pl.when(when)(wait)
 
         return prepare, finish
 
@@ -233,6 +291,9 @@
         inner = (jnp.where(is_b, plus, minus), r)
         outer = (jnp.where(is_b, minus, plus), r)
         sibling = (jnp.where(is_b, slab_at(-4), slab_at(4)), r)
+        has_outer = has_plus
+        has_sibling = jnp.where(is_b, slab >= 4, slab < slabs - 4)
+        has_second = jnp.logical_or(jnp.logical_not(is_b), slab < slabs - 4)
         side = jnp.where(is_b, 0, 1)
         prepare, finish = sender(2)
 
@@ -243,23 +304,23 @@
         s_ye = prepare(lambda j, s: copy(ye, yein.at[side], s, R_YE + side, inner))
         s_cc = prepare(lambda j, s: copy(cc_own, cc_oth, s, R_CCP, partner))
         s_d = prepare(lambda j, s: copy(d_own.at[j], d_oth.at[j], s, R_DP + j, partner), C)
-        s_p = prepare(lambda j, s: copy(p_own.at[j], yin.at[side, j], s, R_YIN + 4 * side + j, outer), C)
+        s_p = prepare(lambda j, s: copy(p_own.at[j], yin.at[side, j], s, R_YIN + 4 * side + j, outer), C, has_outer)
         s_pp = prepare(lambda j, s: copy(p_own.at[j], p_oth.at[j], s, R_P + j, partner), C)
         s_zw = prepare(lambda j, s: copy(x_w.at[j], yin.at[side, j], s, R_ZW + 4 * side + j, inner), C)
-        s_q = prepare(lambda j, s: copy(qv, yein.at[side], s, R_YE + side, outer))
+        s_q = prepare(lambda j, s: copy(qv, yein.at[side], s, R_YE + side, outer), 1, has_outer)
         s_r = prepare(lambda j, s: copy(r_own.at[j], r_oth.at[j], s, R_R + j, partner), C)
 
         def piece(ref, j):
             return ref.at[pl.ds(j * Q, Q), :]
 
-        s_in = prepare(lambda j, s: copy(piece(sin.at[0], j), piece(sin.at[side], j), s, R_S + 4 * side + j, inner), K)
-        s_sib = prepare(lambda j, s: copy(piece(sin.at[0], j), piece(sin.at[1], j), s, R_S + 4 + j, sibling), K)
+        s_in = prepare(lambda j, s: copy(piece(sin.at[0], j), piece(sin.at[side], j), s, R_S + 4 * side + j, inner), K, has_outer)
+        s_sib = prepare(lambda j, s: copy(piece(sin.at[0], j), piece(sin.at[1], j), s, R_S + 4 + j, sibling), K, has_sibling)
 
         stack_rows(st_send.at[0], 0, tw.at[0], other, 0.2)
         s_ci()
         stack_rows(x_ci, mine, tw.at[0], mine, 0.2)
         arrived(a_oth, R_A)
-        split_rows(lhs.at[0], a_ref, mine, True, 3)
+        split_rows(lhs.at[0], a_own, mine, True, 3)
         split_rows(lhs.at[0], a_oth, other, True, 3)
         square(lhs.at[0], lhs.at[1], 3)
         arrived(x_ci.at[:, pl.ds(other, H), :], R_CI)
@@ -287,15 +348,17 @@
         def _(j):
             series(lhs, x_co.at[j], va, vb, True)
 
+        arrived(t_oth, R_CT)
+        choose(t_oth)
         arrived(cc_own, R_CC)
         s_cc()
-        split_rows(lc.at[0], cc_own, mine, False, 2)
+        twist_rows(lc.at[0], cc_own, mine)
         split_chunks(lc.at[1], x_ci, mine, False, 2)
         for j in range(C):
             arrived(y_oth.at[j], R_YCI + j)
         split_chunks(lc.at[1], y_oth, other, False, 2)
         arrived(cc_oth, R_CCP)
-        split_rows(lc.at[0], cc_oth, other, False, 2)
+        twist_rows(lc.at[0], cc_oth, other)
 
         @pl.loop(0, C)
         def _(j):
@@ -343,14 +406,22 @@
             arrived(r_oth.at[j], R_R + j)
         split_chunks(lc.at[0], r_oth, other, False, 2)
 
-        for j in range(K):
-            arrived(piece(sin.at[0], j), R_S + j)
-            s_in(j)
-            s_sib(j)
-        put(va, lc.at[2], sin.at[0], qv, -1.0)
-        for j in range(K):
-            arrived(piece(sin.at[1], j), R_S + 4 + j)
-        put(res, lc.at[0], sin.at[1], va, -1.0)
+        res[...] = qv[...]
+
+        @pl.when(has_outer)
+        def _():
+            for j in range(K):
+                arrived(piece(sin.at[0], j), R_S + j)
+                s_in(j)
+                s_sib(j)
+            put(res, lc.at[2], sin.at[0], res, -1.0)
+
+        @pl.when(has_second)
+        def _():
+            for j in range(K):
+                arrived(piece(sin.at[1], j), R_S + 4 + j)
+            put(res, lc.at[0], sin.at[1], res, -1.0)
+
         finish()
 
     @pl.when(jnp.logical_not(odd))
@@ -366,7 +437,6 @@
 
         s_t = prepare(lambda j, s: copy(tw.at[j], tw_oth.at[j], s, R_T + j, partner), 2)
         s_d = prepare(lambda j, s: copy(d_own.at[j], d_oth.at[j], s, R_DP + j, partner), C)
-        s_cc = [prepare_c(lambda j, s, i=i: copy(tw.at[i], cc_own, s, R_CC, sides[i])) for i in range(2)]
         s_dc = [prepare_c(lambda j, s, i=i: copy(d_own.at[j], d_own.at[j], s, R_D + j, sides[i]), C) for i in range(2)]
         s_zb = [prepare_c(lambda j, s, i=i: copy(zb, zb, s, R_ZB, sides[i])) for i in range(2)]
         s_zwp = [
@@ -376,20 +446,17 @@
         s_zwx = [
             prepare_c(lambda j, s, i=i: copy(yin.at[i, j], zwx.at[j], s, R_ZWX + j, sides[1 - i]), C) for i in range(2)
         ]
+        place = jnp.where(slab == 0, 1, 0)
+        below = (jnp.where(slab == 0, slab_at(3), minus), r)
         s_sa = [
-            prepare_a(lambda j, s, i=i: copy(piece(zb, j), piece(sin.at[0], j), s, R_S + j, sides[i]), K)
-            for i in range(2)
+            prepare_a(lambda j, s: copy(piece(zb, j), piece(sin.at[0], j), s, R_S + j, sides[0]), K),
+            prepare_a(lambda j, s: copy(piece(zb, j), piece(sin.at[place], j), s, R_S + 4 * place + j, below), K),
         ]
 
         for i in range(2):
             s_t(i)
-
-            @pl.when(is_c)
-            def _():
-                s_cc[i]()
-
             split_rows(lc.at[i], tw.at[i], mine, False, 2)
-        stack_rows(a_st, mine, a_ref, mine, 1.0)
+        stack_rows(a_st, mine, a_own, mine, 1.0)
         arrived(a_oth, R_A)
         stack_rows(a_st, other, a_oth, mine, 1.0)
         for i in range(2):
@@ -401,8 +468,11 @@
         def _(j):
             arrived(yin.at[0, j], R_YIN + j)
             put(d_own.at[j], lc.at[0], yin.at[0, j], a_st.at[j], -1.0)
-            arrived(yin.at[1, j], R_YIN + 4 + j)
-            put(d_own.at[j], lc.at[1], yin.at[1, j], d_own.at[j], -1.0)
+
+            @pl.when(has_minus)
+            def _():
+                arrived(yin.at[1, j], R_YIN + 4 + j)
+                put(d_own.at[j], lc.at[1], yin.at[1, j], d_own.at[j], -1.0)
 
             @pl.when(is_c)
             def _():
@@ -417,8 +487,11 @@
         split_chunks(lhs.at[0], d_oth, other, True, 3)
         square(lhs.at[0], lhs.at[1], 2)
         for i in range(2):
-            arrived(yein.at[i], R_YE + i)
-            put(es, lc.at[i], yein.at[i], es, -1.0)
+            @pl.when(slab >= i)
+            def _():
+                arrived(yein.at[i], R_YE + i)
+                put(es, lc.at[i], yein.at[i], es, -1.0)
+
         zb[...] = 0.2 * es[...]
         series(lhs, zb, va, vb, False)
 
@@ -440,11 +513,17 @@
                 for j in range(C):
                     arrived(zwo.at[i, j], R_ZWP + 4 * i + j)
                 split_chunks(lc.at[i], zwo.at[i], other, False, 2)
+            res[...] = zb[...]
             for i in range(2):
-                for j in range(K):
-                    arrived(piece(sin.at[i], j), R_S + 4 * i + j)
-                put(res, lc.at[i], sin.at[i], zb if i == 0 else res)
+                @pl.when(slab < slabs - 1 - i)
+                def _():
+                    for j in range(K):
+                        arrived(piece(sin.at[i], j), R_S + 4 * i + j)
+                    put(res, lc.at[i], sin.at[i], res)
+
             finish_c()
+            for c in couplings:
+                c.wait_send()
 
         @pl.when(jnp.logical_not(is_c))
         def _():
@@ -482,9 +561,11 @@
         out = pl.pallas_call(
             functools.partial(kernel, slabs),
             out_shape=jax.ShapeDtypeStruct((2, H, Q), F32),
-            in_specs=[vmem] * 5,
+            in_specs=[pl.BlockSpec(memory_space=pl.ANY)] * 5,
             out_specs=vmem,
             scratch_shapes=[
+                rows, rows, rows, f32(2, H, Q),
+                pltpu.VMEM((1, N), jnp.int32), pltpu.VMEM((1, N), jnp.int32),
                 pltpu.VMEM((N, N), BF16),
                 f32(2, 2, H, N), rows, f32(2, 2, H, N),
                 chunks, f32(2, C, H, Q),
@@ -498,8 +579,9 @@
                 f32(2, N, Q), f32(H, Q),
                 pltpu.VMEM((3, 3, 2, N, N), BF16),
                 pltpu.VMEM((3, 2, 2, N, N), BF16),
-                pltpu.SemaphoreType.DMA((N_SEND + 1,)),
+                pltpu.SemaphoreType.DMA((N_SEND + 5,)),
                 pltpu.SemaphoreType.DMA((N_RECV,)),
+                pltpu.SemaphoreType.DMA((5,)),
             ],
             compiler_params=pltpu.CompilerParams(
                 collective_id=0, has_side_effects=True, vmem_limit_bytes=60 * 1024 * 1024

time: 128 us -> 119 us (0.930)
  the two profiles are of different devices: /device:TPU:7 before, /device:TPU:103 now
where the time goes in v3:
time: 119 us
  Pallas kernels  117 us (98%)
  local copies, waits for them, and re-layouts  1.67 us (1%)
    pallas_call x1, Pallas kernels, body(): pl.pallas_call(functools.partial(kernel, slabs), out_shape=jax.ShapeDtype...  117 us

profile of v3, /device:TPU:103, one launch (start us, length us, event | category | flops | bytes accessed | tf_op | source)
XLA Modules:
  0.0 118.6 jit_solution(14653604539034400713)
XLA Ops:
  0.0 116.9 %shard_map.55 = f32[2,256,128]{2,1,0:T(8,128)} custom-call(f32[2,256,512]{2,1,0:T(8,128)} %bitcast.5, f32[2,256,512]{2,1,0:T(8,128)} %bitcast.6, f32[2,256,512]{2,1,0:T(8,128)} %bitcast.7, s32[1,512]{1,0:T(1,128)} %tw_ref.1, f32[2,256,128]{2,1,0:T(8,128)} %bitcast.9), custom_call_target="tpu_custom_call" | custom-call | tf_op jit(solution)/shard_map/pallas_call | solution.py:561
  116.9 1.7 %copy.7 = f32[1,2,256,128]{3,2,1,0:T(8,128)} copy(f32[1,2,256,128]{3,2,1,0:T(8,128)} %bitcast.8) | data formatting | bytes 524288

commit v4 on v3

--- a/solution.py
+++ b/solution.py
@@ -15,13 +15,13 @@
 C = 4
 K = 4
 
-R_A, R_E, R_T, R_CI, R_CO, R_CC, R_CCP, R_FIN, R_ZB = 0, 1, 2, 4, 5, 6, 7, 8, 9
+R_A, R_E, R_T, R_CI, R_CO, R_FIN, R_ZB = 0, 1, 2, 4, 5, 8, 9
 R_YE = 10
 R_YCI, R_D, R_DP, R_P, R_R, R_ZWX = 12, 16, 20, 24, 28, 32
-R_YIN, R_ZW, R_ZWP, R_S = 36, 44, 52, 60
-R_CT = 68
-N_RECV = 69
-N_SEND = 64
+R_YIN, R_ZWP, R_S = 36, 52, 60
+R_W, R_YCO = 76, 80
+N_RECV = 88
+N_SEND = 72
 
 
 def dot(a, b):
@@ -77,13 +77,16 @@
             wide = dot(lhs[plane, 0, rs, :], both)
             out.append(wide[:, :Q] + wide[:, Q:] + dot(lhs[plane, 1, rs, :], high))
         turned = turn(out[1])
-        emit(rs, out[0] + jnp.where(lane_low((H, Q)), -turned, turned))
-
-
-def put(dst, lhs, src, base=None, scale=1.0):
-    def emit(rs, value):
+        emit(t, out[0] + jnp.where(lane_low((H, Q)), -turned, turned))
+
+
+def put(dst, lhs, src, base=None, scale=1.0, ready=None):
+    def emit(t, value):
+        rs = pl.ds(t * H, H)
         value = value if scale == 1.0 else scale * value
         dst[rs, :] = value if base is None else base[rs, :] + value
+        if ready is not None:
+            ready(t)
 
     vector_product(lhs, src, emit)
 
@@ -130,29 +133,26 @@
             dst[2 * m + 1, ds, :] = scale * second
 
 
-def square(src, dst, planes):
+def square(src, dst):
     @pl.loop(0, 4)
     def _(t):
         rs = pl.ds(pl.multiple_of((t // 2) * H, H), H)
         cs = pl.ds(pl.multiple_of((t % 2) * H, H), H)
         re, im = product3(src, rs, src, cs)
-        put_split(dst, rs, cs, re, im, planes)
-
-
-def series(lhs, x, va, vb, fourth):
-    put(va, lhs.at[0], x, x)
+        put_split(dst, rs, cs, re, im, 2)
+
+
+def series(lhs, src, dst, va, vb, ready=None):
+    put(va, lhs.at[0], src, src)
     put(vb, lhs.at[1], va, va)
-    if fourth:
-        put(x, lhs.at[2], vb, vb)
-    else:
-        put(va, lhs.at[1], vb)
-        put(x, lhs.at[1], va, vb)
+    put(va, lhs.at[1], vb)
+    put(dst, lhs.at[1], va, vb, ready=ready)
 
 
 def kernel(
     slabs,
     a_ref, l_ref, u_ref, tw_ref, e_ref, o_ref,
-    a_own, l_own, u_own, e_own, t_own, t_oth, onehot, tw, a_oth, tw_oth, a_st, st_send, x_ci, x_co, x_w, y_oth, cc_own, cc_oth,
+    a_own, lu_own, e_own, t_own, onehot, tw, a_oth, tw_oth, a_st, st_send, x_ci, x_co, x_w, y_oth, wco,
     d_own, d_oth, p_own, p_oth, zwx, r_own, r_oth, yin, zwo, yein, es, e_send,
     va, vb, ye, zb, qv, res, sin, fin, lhs, lc, send_sem, recv_sem, load_sem,
 ):
@@ -162,7 +162,7 @@
     odd = lax.rem(role, 2) == 1
 
     loads = []
-    for k, (src, dst) in enumerate(((a_ref, a_own), (tw_ref, t_own), (l_ref, l_own), (u_ref, u_own), (e_ref, e_own))):
+    for k, (src, dst) in enumerate(((a_ref, a_own), (tw_ref, t_own), (l_ref, lu_own.at[0]), (u_ref, lu_own.at[1]), (e_ref, e_own))):
         load = pltpu.make_async_copy(src, dst, load_sem.at[k])
         load.start()
         loads.append(load)
@@ -206,16 +206,6 @@
 
     c_a = copy(a_ref, a_oth, 0, R_A, partner)
     c_a.start()
-    couplings = []
-    for i, (src, where) in enumerate(((l_ref, (minus, r)), (u_ref, (plus, r)))):
-        couplings.append(copy(tw_ref, t_oth, N_SEND + 1 + 2 * i, R_CT, where))
-        couplings.append(copy(src, cc_own, N_SEND + 2 + 2 * i, R_CC, where))
-
-    @pl.when(role == 2)
-    def _():
-        for c in couplings:
-            c.start()
-
     for load in loads:
         load.wait()
 
@@ -228,31 +218,22 @@
     c_e.start()
     es[pl.ds(mine, H), :] = stacked(r)
 
-    def choose(order):
-        @pl.loop(0, N // 64)
-        def _(t):
-            s0 = pl.multiple_of(t * 64, 64)
-            hit = lax.broadcasted_iota(jnp.int32, (64, N), 0) + s0 == order[...]
-            onehot[pl.ds(s0, 64), :] = hit.astype(F32).astype(BF16)
-
-    choose(t_own)
-
-    place_l = 1 - role // 2
-    keep_l = (slab > 0).astype(F32)
-    keep_u = (slab < slabs - 1).astype(F32)
-    for src, place, keep in ((l_own, place_l, keep_l), (u_own, 1 - place_l, keep_u)):
+    @pl.loop(0, N // 64)
+    def _(t):
+        s0 = pl.multiple_of(t * 64, 64)
+        hit = lax.broadcasted_iota(jnp.int32, (64, N), 0) + s0 == t_own[...]
+        onehot[pl.ds(s0, 64), :] = hit.astype(F32).astype(BF16)
+
+    def twist(i):
+        which = 1 - role // 2 if i == 0 else role // 2
+        keep = jnp.where(which == 0, slab > 0, slab < slabs - 1).astype(F32)
+
         @pl.loop(0, 2)
         def _(t):
-            high, low = halves(src[t])
-            tw[place, t] = (dot(high, onehot[...]) + dot(low, onehot[...])) * keep
-
-    def twist_rows(dst, src, row0):
-        rs = pl.ds(row0, H)
-
-        @pl.loop(0, 2)
-        def _(t):
-            for part, value in enumerate(halves(src[t])):
-                dst[t, part, rs, :] = dot(value, onehot[...]).astype(BF16)
+            high, low = halves(lu_own[which, t])
+            tw[i, t] = (dot(high, onehot[...]) + dot(low, onehot[...])) * keep
+
+    twist(0)
 
     def sender(first):
         count = [first]
@@ -302,68 +283,53 @@
         s_yci = prepare(lambda j, s: copy(x_ci.at[j], yin.at[side, j], s, R_YIN + 4 * side + j, inner), C)
         s_ycip = prepare(lambda j, s: copy(x_ci.at[j], y_oth.at[j], s, R_YCI + j, partner), C)
         s_ye = prepare(lambda j, s: copy(ye, yein.at[side], s, R_YE + side, inner))
-        s_cc = prepare(lambda j, s: copy(cc_own, cc_oth, s, R_CCP, partner))
+        s_yco = prepare(lambda j, s: copy(x_co.at[j], wco.at[side, j], s, R_YCO + 4 * side + j, inner), C)
         s_d = prepare(lambda j, s: copy(d_own.at[j], d_oth.at[j], s, R_DP + j, partner), C)
         s_p = prepare(lambda j, s: copy(p_own.at[j], yin.at[side, j], s, R_YIN + 4 * side + j, outer), C, has_outer)
         s_pp = prepare(lambda j, s: copy(p_own.at[j], p_oth.at[j], s, R_P + j, partner), C)
-        s_zw = prepare(lambda j, s: copy(x_w.at[j], yin.at[side, j], s, R_ZW + 4 * side + j, inner), C)
         s_q = prepare(lambda j, s: copy(qv, yein.at[side], s, R_YE + side, outer), 1, has_outer)
         s_r = prepare(lambda j, s: copy(r_own.at[j], r_oth.at[j], s, R_R + j, partner), C)
 
         def piece(ref, j):
-            return ref.at[pl.ds(j * Q, Q), :]
-
-        s_in = prepare(lambda j, s: copy(piece(sin.at[0], j), piece(sin.at[side], j), s, R_S + 4 * side + j, inner), K, has_outer)
-        s_sib = prepare(lambda j, s: copy(piece(sin.at[0], j), piece(sin.at[1], j), s, R_S + 4 + j, sibling), K, has_sibling)
+            return ref.at[pl.ds(j * (N // K), N // K), :]
+
+        s_in = prepare(lambda j, s: copy(piece(sin.at[0], j), piece(sin.at[side], j), s, R_S + K * side + j, inner), K, has_outer)
+        s_sib = prepare(lambda j, s: copy(piece(sin.at[0], j), piece(sin.at[1], j), s, R_S + K + j, sibling), K, has_sibling)
 
         stack_rows(st_send.at[0], 0, tw.at[0], other, 0.2)
         s_ci()
         stack_rows(x_ci, mine, tw.at[0], mine, 0.2)
+        split_rows(lhs.at[0], a_own, mine, True, 3)
         arrived(a_oth, R_A)
-        split_rows(lhs.at[0], a_own, mine, True, 3)
         split_rows(lhs.at[0], a_oth, other, True, 3)
-        square(lhs.at[0], lhs.at[1], 3)
+        square(lhs.at[0], lhs.at[1])
         arrived(x_ci.at[:, pl.ds(other, H), :], R_CI)
-        series(lhs, x_ci.at[0], va, vb, False)
-        s_yci(0)
-        s_ycip(0)
-        square(lhs.at[1], lhs.at[2], 2)
-
-        @pl.loop(1, C)
+
+        @pl.loop(0, C)
         def _(j):
-            series(lhs, x_ci.at[j], va, vb, True)
+            series(lhs, x_ci.at[j], x_ci.at[j], va, vb)
             s_yci(j)
             s_ycip(j)
 
+        twist(1)
         stack_rows(st_send.at[1], 0, tw.at[1], other, 0.2)
         s_co()
         stack_rows(x_co, mine, tw.at[1], mine, 0.2)
+        arrived(x_co.at[:, pl.ds(other, H), :], R_CO)
+
+        @pl.loop(0, C)
+        def _(j):
+            series(lhs, x_co.at[j], x_co.at[j], va, vb)
+            s_yco(j)
+
         arrived(es.at[pl.ds(other, H), :], R_E)
         ye[...] = 0.2 * es[...]
-        series(lhs, ye, va, vb, True)
+        series(lhs, ye, ye, va, vb)
         s_ye()
-        arrived(x_co.at[:, pl.ds(other, H), :], R_CO)
-
-        @pl.loop(0, C)
-        def _(j):
-            series(lhs, x_co.at[j], va, vb, True)
-
-        arrived(t_oth, R_CT)
-        choose(t_oth)
-        arrived(cc_own, R_CC)
-        s_cc()
-        twist_rows(lc.at[0], cc_own, mine)
         split_chunks(lc.at[1], x_ci, mine, False, 2)
         for j in range(C):
             arrived(y_oth.at[j], R_YCI + j)
         split_chunks(lc.at[1], y_oth, other, False, 2)
-        arrived(cc_oth, R_CCP)
-        twist_rows(lc.at[0], cc_oth, other)
-
-        @pl.loop(0, C)
-        def _(j):
-            put(x_w.at[j], lc.at[0], x_co.at[j], scale=0.2)
-
         for j in range(C):
             arrived(d_own.at[j], R_D + j)
             s_d(j)
@@ -371,21 +337,15 @@
         for j in range(C):
             arrived(d_oth.at[j], R_DP + j)
         split_chunks(lhs.at[0], d_oth, other, True, 3)
-        square(lhs.at[0], lhs.at[1], 3)
-
-        def reduced(j, fourth):
-            series(lhs, x_w.at[j], va, vb, fourth)
-            s_zw(j)
+        square(lhs.at[0], lhs.at[1])
+
+        @pl.loop(0, C)
+        def _(j):
+            arrived(x_w.at[j], R_W + j)
+            series(lhs, x_w.at[j], x_w.at[j], va, vb)
             put(p_own.at[j], lc.at[1], x_w.at[j], x_co.at[j])
             s_p(j)
             s_pp(j)
-
-        reduced(0, False)
-        square(lhs.at[1], lhs.at[2], 2)
-
-        @pl.loop(1, C)
-        def _(j):
-            reduced(j, True)
 
         arrived(zb, R_ZB)
         put(qv, lc.at[1], zb, ye, -1.0)
@@ -419,7 +379,7 @@
         @pl.when(has_second)
         def _():
             for j in range(K):
-                arrived(piece(sin.at[1], j), R_S + 4 + j)
+                arrived(piece(sin.at[1], j), R_S + K + j)
             put(res, lc.at[0], sin.at[1], res, -1.0)
 
         finish()
@@ -433,29 +393,33 @@
         prepare_a, finish_a = sender(24)
 
         def piece(ref, j):
-            return ref.at[pl.ds(j * Q, Q), :]
+            return ref.at[pl.ds(j * (N // K), N // K), :]
 
         s_t = prepare(lambda j, s: copy(tw.at[j], tw_oth.at[j], s, R_T + j, partner), 2)
         s_d = prepare(lambda j, s: copy(d_own.at[j], d_oth.at[j], s, R_DP + j, partner), C)
         s_dc = [prepare_c(lambda j, s, i=i: copy(d_own.at[j], d_own.at[j], s, R_D + j, sides[i]), C) for i in range(2)]
+        s_w = [prepare_c(lambda j, s, i=i: copy(wco.at[i, j], x_w.at[j], s, R_W + j, sides[i]), C) for i in range(2)]
         s_zb = [prepare_c(lambda j, s, i=i: copy(zb, zb, s, R_ZB, sides[i])) for i in range(2)]
-        s_zwp = [
-            prepare_c(lambda j, s, i=i: copy(yin.at[i, j], zwo.at[i, j], s, R_ZWP + 4 * i + j, partner), C)
-            for i in range(2)
-        ]
-        s_zwx = [
-            prepare_c(lambda j, s, i=i: copy(yin.at[i, j], zwx.at[j], s, R_ZWX + j, sides[1 - i]), C) for i in range(2)
-        ]
+        def pair(ref, m):
+            return ref.at[m % 2, m // 2]
+
+        def opposite(m):
+            return (jnp.where(m % 2 == 0, sides[1][0], sides[0][0]), r)
+
+        s_zwp = prepare_c(lambda m, s: copy(pair(yin, m), pair(zwo, m), s, R_ZWP + m, partner), 2 * C)
+        s_zwx = prepare_c(lambda m, s: copy(pair(yin, m), zwx.at[m // 2], s, R_ZWX + m // 2, opposite(m)), 2 * C)
         place = jnp.where(slab == 0, 1, 0)
         below = (jnp.where(slab == 0, slab_at(3), minus), r)
         s_sa = [
             prepare_a(lambda j, s: copy(piece(zb, j), piece(sin.at[0], j), s, R_S + j, sides[0]), K),
-            prepare_a(lambda j, s: copy(piece(zb, j), piece(sin.at[place], j), s, R_S + 4 * place + j, below), K),
+            prepare_a(lambda j, s: copy(piece(zb, j), piece(sin.at[place], j), s, R_S + K * place + j, below), K),
         ]
 
+        twist(1)
         for i in range(2):
             s_t(i)
             split_rows(lc.at[i], tw.at[i], mine, False, 2)
+
         stack_rows(a_st, mine, a_own, mine, 1.0)
         arrived(a_oth, R_A)
         stack_rows(a_st, other, a_oth, mine, 1.0)
@@ -485,7 +449,33 @@
         for j in range(C):
             arrived(d_oth.at[j], R_DP + j)
         split_chunks(lhs.at[0], d_oth, other, True, 3)
-        square(lhs.at[0], lhs.at[1], 2)
+
+        def couple(j):
+            for i in range(2):
+                arrived(wco.at[i, j], R_YCO + 4 * i + j)
+                put(wco.at[i, j], lc.at[i], wco.at[i, j], scale=0.2)
+                s_w[i](j)
+
+        def inverted(m):
+            series(lhs, pair(wco, m), pair(yin, m), va, vb)
+            s_zwp(m)
+
+        @pl.when(is_c)
+        def _():
+            couple(0)
+
+        square(lhs.at[0], lhs.at[1])
+
+        @pl.when(is_c)
+        def _():
+            @pl.loop(1, C)
+            def _(j):
+                couple(j)
+                inverted(j - 1)
+
+            s_zwx(0)
+            s_zwx(1)
+
         for i in range(2):
             @pl.when(slab >= i)
             def _():
@@ -493,43 +483,46 @@
                 put(es, lc.at[i], yein.at[i], es, -1.0)
 
         zb[...] = 0.2 * es[...]
-        series(lhs, zb, va, vb, False)
+
+        def send_tile(t):
+            @pl.when(jnp.logical_not(is_c))
+            def _():
+                for j in range(t * K // 2, (t + 1) * K // 2):
+                    for i in range(2):
+                        s_sa[i](j)
+
+        series(lhs, zb, zb, va, vb, send_tile)
 
         @pl.when(is_c)
         def _():
             for i in range(2):
                 s_zb[i]()
 
-            @pl.loop(0, C)
-            def _(j):
-                for i in range(2):
-                    arrived(yin.at[i, j], R_ZW + 4 * i + j)
-                    s_zwx[i](j)
-                    s_zwp[i](j)
+            s_zwx(2)
+
+            @pl.loop(C - 1, 2 * C)
+            def _(m):
+                inverted(m)
+                s_zwx(m)
 
             for i in range(2):
                 split_chunks(lc.at[i], yin.at[i], mine, False, 2)
             for i in range(2):
                 for j in range(C):
-                    arrived(zwo.at[i, j], R_ZWP + 4 * i + j)
+                    arrived(zwo.at[i, j], R_ZWP + 2 * j + i)
                 split_chunks(lc.at[i], zwo.at[i], other, False, 2)
             res[...] = zb[...]
             for i in range(2):
                 @pl.when(slab < slabs - 1 - i)
                 def _():
                     for j in range(K):
-                        arrived(piece(sin.at[i], j), R_S + 4 * i + j)
+                        arrived(piece(sin.at[i], j), R_S + K * i + j)
                     put(res, lc.at[i], sin.at[i], res)
 
             finish_c()
-            for c in couplings:
-                c.wait_send()
 
         @pl.when(jnp.logical_not(is_c))
         def _():
-            for j in range(K):
-                for i in range(2):
-                    s_sa[i](j)
             res[...] = zb[...]
             finish_a()
 
@@ -564,22 +557,22 @@
             in_specs=[pl.BlockSpec(memory_space=pl.ANY)] * 5,
             out_specs=vmem,
             scratch_shapes=[
-                rows, rows, rows, f32(2, H, Q),
-                pltpu.VMEM((1, N), jnp.int32), pltpu.VMEM((1, N), jnp.int32),
+                rows, f32(2, 2, H, N), f32(2, H, Q),
+                pltpu.VMEM((1, N), jnp.int32),
                 pltpu.VMEM((N, N), BF16),
                 f32(2, 2, H, N), rows, f32(2, 2, H, N),
                 chunks, f32(2, C, H, Q),
                 chunks, chunks, chunks, chunks,
-                rows, rows,
+                f32(2, C, N, Q),
                 chunks, chunks, chunks, chunks,
                 chunks, chunks, chunks,
                 f32(2, C, N, Q), f32(2, C, N, Q), f32(2, N, Q),
                 vector, f32(H, Q),
                 vector, vector, vector, vector, vector, vector,
                 f32(2, N, Q), f32(H, Q),
-                pltpu.VMEM((3, 3, 2, N, N), BF16),
+                pltpu.VMEM((2, 3, 2, N, N), BF16),
                 pltpu.VMEM((3, 2, 2, N, N), BF16),
-                pltpu.SemaphoreType.DMA((N_SEND + 5,)),
+                pltpu.SemaphoreType.DMA((N_SEND + 1,)),
                 pltpu.SemaphoreType.DMA((N_RECV,)),
                 pltpu.SemaphoreType.DMA((5,)),
             ],

time: 119 us -> 114 us (0.958)
  Pallas kernels: 117 us -> 113 us
    pallas_call x1, Pallas kernels: 117 us -> 113 us  [body(): pl.pallas_call(functools.partial(kernel, slabs), out_shape=jax.ShapeDtype...]
where the time goes in v4:
time: 114 us
  Pallas kernels  113 us (99%)
  local copies, waits for them, and re-layouts  1.67 us (1%)
    pallas_call x1, Pallas kernels, body(): pl.pallas_call(functools.partial(kernel, slabs), out_shape=jax.ShapeDtype...  113 us

profile of v4, /device:TPU:103, one launch (start us, length us, event | category | flops | bytes accessed | tf_op | source)
XLA Modules:
  0.0 114.4 jit_solution(2298630616512505769)
XLA Ops:
  0.0 112.7 %shard_map.55 = f32[2,256,128]{2,1,0:T(8,128)} custom-call(f32[2,256,512]{2,1,0:T(8,128)} %bitcast.5, f32[2,256,512]{2,1,0:T(8,128)} %bitcast.6, f32[2,256,512]{2,1,0:T(8,128)} %bitcast.7, s32[1,512]{1,0:T(1,128)} %tw_ref.1, f32[2,256,128]{2,1,0:T(8,128)} %bitcast.9), custom_call_target="tpu_custom_call" | custom-call | tf_op jit(solution)/shard_map/pallas_call | solution.py:554
  112.7 1.7 %copy.7 = f32[1,2,256,128]{3,2,1,0:T(8,128)} copy(f32[1,2,256,128]{3,2,1,0:T(8,128)} %bitcast.8) | data formatting | bytes 524288

commit v5 on v4

--- a/solution.py
+++ b/solution.py
@@ -13,7 +13,7 @@
 H = 256
 Q = 128
 C = 4
-K = 4
+K = 8
 
 R_A, R_E, R_T, R_CI, R_CO, R_FIN, R_ZB = 0, 1, 2, 4, 5, 8, 9
 R_YE = 10
@@ -67,28 +67,27 @@
     return jnp.where(low, first, turn(second)), jnp.where(low, turn(first), second)
 
 
-def vector_product(lhs, stack_ref, emit):
+def vector_product(lhs, stack_ref, emit, flip=None):
     high, low = halves(stack_ref[...])
     both = jnp.concatenate([high, low], axis=1)
     for t in range(N // H):
-        rs = pl.ds(t * H, H)
+        rs = pl.ds(t * H if flip is None else pl.multiple_of((t + flip) % 2 * H, H), H)
         out = []
         for plane in range(2):
             wide = dot(lhs[plane, 0, rs, :], both)
             out.append(wide[:, :Q] + wide[:, Q:] + dot(lhs[plane, 1, rs, :], high))
         turned = turn(out[1])
-        emit(t, out[0] + jnp.where(lane_low((H, Q)), -turned, turned))
-
-
-def put(dst, lhs, src, base=None, scale=1.0, ready=None):
-    def emit(t, value):
-        rs = pl.ds(t * H, H)
+        emit(t, rs, out[0] + jnp.where(lane_low((H, Q)), -turned, turned))
+
+
+def put(dst, lhs, src, base=None, scale=1.0, ready=None, flip=None):
+    def emit(t, rs, value):
         value = value if scale == 1.0 else scale * value
         dst[rs, :] = value if base is None else base[rs, :] + value
         if ready is not None:
             ready(t)
 
-    vector_product(lhs, src, emit)
+    vector_product(lhs, src, emit, flip)
 
 
 def identity_minus(re, im, row0, col0):
@@ -234,6 +233,13 @@
             tw[i, t] = (dot(high, onehot[...]) + dot(low, onehot[...])) * keep
 
     twist(0)
+
+    c_f = copy(res.at[pl.ds(other, H), :], fin, N_SEND, R_FIN, partner)
+    early = jnp.where(odd, jnp.logical_or(role == 3, slab < slabs - 4), jnp.logical_and(role == 2, slab < slabs - 2))
+
+    def hand_over(t):
+        if t == 0:
+            c_f.start()
 
     def sender(first):
         count = [first]
@@ -355,32 +361,39 @@
             arrived(p_oth.at[j], R_P + j)
         split_chunks(lc.at[2], p_oth, other, False, 2)
 
-        @pl.loop(0, C)
-        def _(j):
+        def second(j):
             arrived(zwx.at[j], R_ZWX + j)
             put(r_own.at[j], lc.at[1], zwx.at[j])
             s_r(j)
 
+        def relay(first, last):
+            @pl.when(has_outer)
+            def _():
+                for j in range(first, last):
+                    arrived(piece(sin.at[0], j), R_S + j)
+                    s_in(j)
+                    s_sib(j)
+
+        pl.loop(0, C - 1)(second)
+        relay(0, K // 2)
+        second(C - 1)
+        relay(K // 2, K)
         split_chunks(lc.at[0], r_own, mine, False, 2)
+        res[...] = qv[...]
+
+        @pl.when(has_outer)
+        def _():
+            put(res, lc.at[2], sin.at[0], res, -1.0)
+
         for j in range(C):
             arrived(r_oth.at[j], R_R + j)
         split_chunks(lc.at[0], r_oth, other, False, 2)
-
-        res[...] = qv[...]
-
-        @pl.when(has_outer)
-        def _():
-            for j in range(K):
-                arrived(piece(sin.at[0], j), R_S + j)
-                s_in(j)
-                s_sib(j)
-            put(res, lc.at[2], sin.at[0], res, -1.0)
 
         @pl.when(has_second)
         def _():
             for j in range(K):
                 arrived(piece(sin.at[1], j), R_S + K + j)
-            put(res, lc.at[0], sin.at[1], res, -1.0)
+            put(res, lc.at[0], sin.at[1], res, -1.0, hand_over, 1 - r)
 
         finish()
 
@@ -517,7 +530,7 @@
                 def _():
                     for j in range(K):
                         arrived(piece(sin.at[i], j), R_S + K * i + j)
-                    put(res, lc.at[i], sin.at[i], res)
+                    put(res, lc.at[i], sin.at[i], res, 1.0, hand_over if i else None, 1 - r)
 
             finish_c()
 
@@ -528,8 +541,7 @@
 
         finish()
 
-    c_f = copy(res.at[pl.ds(other, H), :], fin, N_SEND, R_FIN, partner)
-    c_f.start()
+    pl.when(jnp.logical_not(early))(c_f.start)
     own = res[pl.ds(mine, H), :]
     arrived(fin, R_FIN)
     oth = fin[...]

time: 114 us -> 112 us (0.982)
  Pallas kernels: 113 us -> 110 us
    pallas_call x1, Pallas kernels: 113 us -> 110 us  [body(): pl.pallas_call(functools.partial(kernel, slabs), out_shape=jax.ShapeDtype...]
where the time goes in v5:
time: 112 us
  Pallas kernels  110 us (98%)
  local copies, waits for them, and re-layouts  1.67 us (1%)
    pallas_call x1, Pallas kernels, body(): pl.pallas_call(functools.partial(kernel, slabs), out_shape=jax.ShapeDtype...  110 us

profile of v5, /device:TPU:103, one launch (start us, length us, event | category | flops | bytes accessed | tf_op | source)
XLA Modules:
  0.0 111.8 jit_solution(5342882961345592644)
XLA Ops:
  0.0 110.2 %shard_map.55 = f32[2,256,128]{2,1,0:T(8,128)} custom-call(f32[2,256,512]{2,1,0:T(8,128)} %bitcast.5, f32[2,256,512]{2,1,0:T(8,128)} %bitcast.6, f32[2,256,512]{2,1,0:T(8,128)} %bitcast.7, s32[1,512]{1,0:T(1,128)} %tw_ref.1, f32[2,256,128]{2,1,0:T(8,128)} %bitcast.9), custom_call_target="tpu_custom_call" | custom-call | tf_op jit(solution)/shard_map/pallas_call | solution.py:566
  110.2 1.7 %copy.7 = f32[1,2,256,128]{3,2,1,0:T(8,128)} copy(f32[1,2,256,128]{3,2,1,0:T(8,128)} %bitcast.8) | data formatting | bytes 524288

commit v6 on v5

--- a/solution.py
+++ b/solution.py
@@ -13,7 +13,7 @@
 H = 256
 Q = 128
 C = 4
-K = 8
+K = 4
 
 R_A, R_E, R_T, R_CI, R_CO, R_FIN, R_ZB = 0, 1, 2, 4, 5, 8, 9
 R_YE = 10

time: 112 us -> 112 us (level)
  no operation moved by 1% of the time
where the time goes in v6:
time: 112 us
  Pallas kernels  111 us (99%)
  local copies, waits for them, and re-layouts  1.67 us (1%)
    pallas_call x1, Pallas kernels, body(): pl.pallas_call(functools.partial(kernel, slabs), out_shape=jax.ShapeDtype...  111 us

profile of v6, /device:TPU:103, one launch (start us, length us, event | category | flops | bytes accessed | tf_op | source)
XLA Modules:
  0.0 112.2 jit_solution(15965667978781577487)
XLA Ops:
  0.0 110.6 %shard_map.55 = f32[2,256,128]{2,1,0:T(8,128)} custom-call(f32[2,256,512]{2,1,0:T(8,128)} %bitcast.5, f32[2,256,512]{2,1,0:T(8,128)} %bitcast.6, f32[2,256,512]{2,1,0:T(8,128)} %bitcast.7, s32[1,512]{1,0:T(1,128)} %tw_ref.1, f32[2,256,128]{2,1,0:T(8,128)} %bitcast.9), custom_call_target="tpu_custom_call" | custom-call | tf_op jit(solution)/shard_map/pallas_call | solution.py:566
  110.6 1.7 %copy.7 = f32[1,2,256,128]{3,2,1,0:T(8,128)} copy(f32[1,2,256,128]{3,2,1,0:T(8,128)} %bitcast.8) | data formatting | bytes 524288
